TPU v7x, 1024 devices: a whole 4x8x16 slice. The times are simulated.
1024 devices in a mesh: seq: 128 (over z, x, core), head: 8 (over y).
Axes of the slice: x: 4, y: 8, z: 16, core: 2. Of those that a mesh axis runs over, the one named last changes fastest.
Arguments:
- grad_out: bfloat16 [16384, 3072], P('seq', 'head'), may hold values from -6 to 6
- out_weight: bfloat16 [3072, 3072], P('head', 'seq'), may hold values from -0.109375 to 0.109375
- row_owner: int32 [16384], P('seq'), may hold values from 0 to 127, as said below
- row_position: int32 [16384], P('seq'), may hold values from 0 to 127, as said below
- query_rows: bfloat16 [16384, 3072], P('seq', 'head'), may hold values from -48 to 48
- key_rows: bfloat16 [16384, 3072], P('seq', 'head'), may hold values from -48 to 48
- value_rows: bfloat16 [16384, 3072], P('seq', 'head'), may hold values from -6 to 6
- band_widths: int32 [128, 2], P('seq'), may hold values from 16 to 64, as said below
Outputs:
- grad_query: bfloat16 [16384, 3072], P('seq', 'head')
- grad_key: bfloat16 [16384, 3072], P('seq', 'head')
- grad_value: bfloat16 [16384, 3072], P('seq', 'head')
Inputs may be any that keep to these rules, and one draw needn't show every extreme that they name: `row_owner`: each frame receives each of its 128 positions from exactly one packed row. One device holds at most 1 row of one frame, and every device holds exactly 1 row of some frame; how many rows device s holds of frame o depends only on (o - s) mod 128, and is at least one for (o - s) mod 128 equal to 1, 64 and 127. `row_position`: together with row_owner, a permutation of all tokens. `band_widths`: column 0 lies in 32 to 64, column 1 in 16 to 32.
All inputs are finite; a program needn't handle non-finite values.
Results may differ from a plain program's by a relative error of at most 0.0088.
Values may be sent and summed in bfloat16 or wider, within the bound.
No kernel may reach another device: no remote copies, remote signals or barrier semaphores. Data moves between devices by JAX's collectives and lax.ppermute only.
A program may use at most 32 MiB of HBM per device.

v0:
```python
import jax
import jax.numpy as jnp
from jax import lax
from jax.sharding import PartitionSpec as P

HEAD_DIM = 128


DISTANCES = (0, 1, 2, 4)
NEG_FILL = -1e30


def shifted(value, axis, by):
    peers = lax.axis_size(axis)
    pairs = [(i, i + by) for i in range(peers) if 0 <= i + by < peers]
    return lax.ppermute(value, axis, pairs)


def per_device(
    grad_out, out_weight, row_owner, row_position, query_rows, key_rows, value_rows, band_widths
):
    frame_len = query_rows.shape[0]
    width = query_rows.shape[1]
    heads = width // HEAD_DIM
    scale = HEAD_DIM ** (-0.5)
    full_grad = lax.all_gather(grad_out, "head", axis=1, tiled=True)
    packed = jnp.einsum(
        "rc,hc->rh",
        full_grad,
        lax.all_gather(out_weight, "seq", axis=1, tiled=True),
        preferred_element_type=jnp.float32,
    ).astype(jnp.bfloat16)
    owners = lax.axis_size("seq")
    capacity = max(1, 3 * frame_len // (2 * owners))
    order_ids = jnp.arange(frame_len)
    same_owner = (row_owner[:, None] == row_owner[None, :]) & (
        order_ids[None, :] < order_ids[:, None]
    )
    earlier = jnp.sum(same_owner.astype(jnp.int32), axis=1)
    slot_ids = row_owner * capacity + earlier
    placing = jnp.arange(owners * capacity)[:, None] == slot_ids[None, :]
    outgoing = jnp.dot(placing.astype(jnp.bfloat16), packed, preferred_element_type=jnp.float32)
    outgoing = outgoing.astype(jnp.bfloat16).reshape(owners, capacity, width)
    slot_pos = (
        jnp.dot(
            placing.astype(jnp.float32),
            (row_position + 1).astype(jnp.float32),
            precision=lax.Precision.HIGHEST,
        )
        - 1.0
    )
    slot_pos = slot_pos.reshape(owners, capacity).astype(jnp.bfloat16)
    incoming, incoming_pos = (
        lax.all_to_all(outgoing, "seq", split_axis=0, concat_axis=0, tiled=True),
        lax.all_to_all(slot_pos, "seq", split_axis=0, concat_axis=0, tiled=True),
    )
    landing = (
        incoming_pos.reshape(-1).astype(jnp.float32)[None, :]
        == jnp.arange(frame_len, dtype=jnp.float32)[:, None]
    )
    grad_attn = jnp.dot(
        landing.astype(jnp.bfloat16),
        incoming.reshape(-1, width),
        preferred_element_type=jnp.float32,
    ).astype(jnp.bfloat16)
    frame = lax.axis_index("seq")
    remote = {}
    for distance in (1, 2, 4):
        remote[distance] = shifted((key_rows, value_rows), "seq", distance)
    remote[0] = (key_rows, value_rows)
    positions = jnp.arange(frame_len)
    spread = jnp.abs(positions[:, None] - positions[None, :])
    limits = {0: frame_len, 1: frame_len, 2: band_widths[0, 0], 4: band_widths[0, 1]}
    mask_list = [(frame - distance >= 0) & (spread < limits[distance]) for distance in DISTANCES]
    usable = jnp.concatenate(mask_list, axis=1)[None]
    key_all = jnp.concatenate([remote[distance][0] for distance in DISTANCES], axis=0)
    value_all = jnp.concatenate([remote[distance][1] for distance in DISTANCES], axis=0)
    key_heads = key_all.reshape(4 * frame_len, heads, HEAD_DIM)
    value_heads = value_all.reshape(4 * frame_len, heads, HEAD_DIM)
    query_heads = query_rows.reshape(frame_len, heads, HEAD_DIM)
    grad_heads = grad_attn.reshape(frame_len, heads, HEAD_DIM)
    scores = (
        jnp.einsum("ihc,jhc->hij", query_heads, key_heads, preferred_element_type=jnp.float32)
        * scale
    )
    row_max = jnp.max(jnp.where(usable, scores, NEG_FILL), axis=2, keepdims=True)
    weights = jnp.where(usable, jnp.exp(scores - row_max), 0.0)
    row_sum = jnp.sum(weights, axis=2, keepdims=True)
    attn_prob = weights / row_sum
    prob_half = attn_prob.astype(jnp.bfloat16)
    attn_out = jnp.einsum(
        "hij,jhc->ihc", prob_half, value_heads, preferred_element_type=jnp.float32
    )
    row_dot = jnp.sum(grad_heads.astype(jnp.float32) * attn_out, axis=2).T[:, :, None]
    grad_prob = jnp.einsum(
        "ihc,jhc->hij", grad_heads, value_heads, preferred_element_type=jnp.float32
    )
    grad_score = (attn_prob * (grad_prob - row_dot)).astype(jnp.bfloat16)
    grad_query = scale * jnp.einsum(
        "hij,jhc->ihc", grad_score, key_heads, preferred_element_type=jnp.float32
    )
    grad_query = grad_query.reshape(frame_len, width).astype(jnp.bfloat16)
    key_terms = scale * jnp.einsum(
        "hij,ihc->jhc", grad_score, query_heads, preferred_element_type=jnp.float32
    )
    key_terms = key_terms.reshape(4, frame_len, width)
    value_terms = jnp.einsum(
        "hij,ihc->jhc", prob_half, grad_heads, preferred_element_type=jnp.float32
    )
    value_terms = value_terms.reshape(4, frame_len, width)
    parts = {}
    for slot, distance in enumerate(DISTANCES):
        parts[distance] = (key_terms[slot], value_terms[slot])
    key_sum, value_sum = parts[0]
    for distance in (1, 2, 4):
        back_key, back_value = shifted(parts[distance], "seq", -distance)
        key_sum = key_sum + back_key
        value_sum = value_sum + back_value
    return (grad_query, key_sum.astype(jnp.bfloat16), value_sum.astype(jnp.bfloat16))


def solution(mesh):
    return jax.shard_map(
        per_device,
        mesh=mesh,
        in_specs=(
            P("seq", "head"),
            P("head", "seq"),
            P("seq"),
            P("seq"),
            P("seq", "head"),
            P("seq", "head"),
            P("seq", "head"),
            P("seq", None),
        ),
        out_specs=(P("seq", "head"), P("seq", "head"), P("seq", "head")),
        check_vma=False,
    )
```

profile of v0, /device:TPU:7, one launch (start us, length us, event | category | flops | bytes accessed | tf_op | source)
XLA Modules:
  0.0 239.5 jit_solution(15581507137441571020)
XLA Ops:
  7.2 0.0 all-gather.2.cloned.1.call-start
  7.2 0.7 all-gather.2.cloned.1.call-update
  7.9 1.0 copy.126
  8.9 4.8 %collective-permute-start.2 = (bf16[128,384]{0,1:T(8,128)(2,1)S(1)}, bf16[128,384]{0,1:T(8,128)(2,1)S(1)}, u32[]{:S(2)}, u32[]{:S(2)}) collective-permute-start(bf16[128,384]{0,1:T(8,128)(2,1)S(1)} %copy.126), channel_id=1, source_target_pairs={{0,32},{8,40},{16,48},{24,56},{32,64},{40,72},{48,80},{56,88},{64,... | collective-permute-start | bytes 294920 | tf_op jit(solution)/shard_map/ppermute | solution.py:16
  13.8 3.7 %collective-permute-start.1 = (bf16[128,384]{0,1:T(8,128)(2,1)S(1)}, bf16[128,384]{0,1:T(8,128)(2,1)S(1)}, u32[]{:S(2)}, u32[]{:S(2)}) collective-permute-start(bf16[128,384]{0,1:T(8,128)(2,1)S(1)} %copy.126), channel_id=1, source_target_pairs={{0,16},{8,24},{16,32},{24,40},{32,48},{40,56},{48,64},{56,72},{64,... | collective-permute-start | bytes 294920 | tf_op jit(solution)/shard_map/ppermute | solution.py:16
  17.5 3.3 %collective-permute-start = (bf16[128,384]{0,1:T(8,128)(2,1)S(1)}, bf16[128,384]{0,1:T(8,128)(2,1)S(1)}, u32[]{:S(2)}, u32[]{:S(2)}) collective-permute-start(bf16[128,384]{0,1:T(8,128)(2,1)S(1)} %copy.126), channel_id=1, source_target_pairs={{0,8},{8,16},{16,24},{24,32},{32,40},{40,48},{48,56},{56,64},{64,7... | collective-permute-start | bytes 294920 | tf_op jit(solution)/shard_map/ppermute | solution.py:16
  20.8 1.0 copy.136
  21.9 4.8 %collective-permute-start.5 = (bf16[128,384]{0,1:T(8,128)(2,1)S(1)}, bf16[128,384]{0,1:T(8,128)(2,1)S(1)}, u32[]{:S(2)}, u32[]{:S(2)}) collective-permute-start(bf16[128,384]{0,1:T(8,128)(2,1)S(1)} %copy.136), channel_id=1, source_target_pairs={{0,32},{8,40},{16,48},{24,56},{32,64},{40,72},{48,80},{56,88},{64,... | collective-permute-start | bytes 294920 | tf_op jit(solution)/shard_map/ppermute | solution.py:16
  26.7 4.3 %collective-permute-start.4 = (bf16[128,384]{0,1:T(8,128)(2,1)S(1)}, bf16[128,384]{0,1:T(8,128)(2,1)S(1)}, u32[]{:S(2)}, u32[]{:S(2)}) collective-permute-start(bf16[128,384]{0,1:T(8,128)(2,1)S(1)} %copy.136), channel_id=1, source_target_pairs={{0,16},{8,24},{16,32},{24,40},{32,48},{40,56},{48,64},{56,72},{64,... | collective-permute-start | bytes 294920 | tf_op jit(solution)/shard_map/ppermute | solution.py:16
  31.0 0.9 convert_reduce_fusion.1
  32.0 0.7 add.31
  32.6 0.8 fusion.15
  33.4 0.8 copy.130
  34.2 20.7 %all-to-all-start = ((bf16[128,1,1]{2,1,0:T(2,128)(2,1)}), bf16[128,1,1]{2,1,0:T(2,128)(2,1)S(1)}, u32[]{:S(2)}, u32[]{:S(2)}) async-start(bf16[128,1,1]{2,1,0:T(2,128)(2,1)} %copy.130), calls=%async_computation | async-start | bytes 131072 | tf_op jit(solution)/shard_map/all_to_all | solution.py:55
  54.9 1.3 fusion.53
  56.3 1.3 fusion.29
  57.6 24.3 %all_gather.6 = bf16[128,3072]{1,0:T(8,128)(2,1)S(1)} all-gather(bf16[128,384]{1,0:T(8,128)(2,1)} %param.8), channel_id=1, replica_groups=mesh['seq'=128,'head'=8] {'head'}, dimensions={1}, use_global_device_ids=true | all-gather | bytes 884736 | tf_op jit(solution)/shard_map/all_gather | solution.py:26
  82.0 1.0 copy.127
  83.0 1.0 convert_reduce_fusion
  84.0 0.0 collective-permute-done.2
  84.0 7.0 %collective-permute-start.3 = (bf16[128,384]{0,1:T(8,128)(2,1)S(1)}, bf16[128,384]{0,1:T(8,128)(2,1)S(1)}, u32[]{:S(2)}, u32[]{:S(2)}) collective-permute-start(bf16[128,384]{0,1:T(8,128)(2,1)S(1)} %copy.136), channel_id=1, source_target_pairs={{0,8},{8,16},{16,24},{24,32},{32,40},{40,48},{48,56},{56,64},{64,7... | collective-permute-start | bytes 294920 | tf_op jit(solution)/shard_map/ppermute | solution.py:16
  91.0 0.0 collective-permute-done.1
  91.1 76.1 %all-gather.2.cloned.1.call-done = bf16[384,3072]{0,1:T(8,128)(2,1)} async-done(((bf16[384,24]{0,1:T(8,128)(2,1)}), bf16[384,3072]{0,1:T(8,128)(2,1)}) %all-gather.2.cloned.1.call-update) | async-done | bytes 2359312 | tf_op jit(solution)/shard_map/all_gather | solution.py:30
  167.3 2.4 fusion.12
  169.6 0.5 broadcast.25
  170.2 0.7 reduce.2
  170.8 0.8 reshape.75
  171.6 12.1 %all-to-all-start.1 = ((bf16[128,2,192]{2,1,0:T(2,128)(2,1)}), bf16[128,2,192]{2,1,0:T(2,128)(2,1)S(1)}, u32[]{:S(2)}, u32[]{:S(2)}) async-start(bf16[128,2,192]{2,1,0:T(2,128)(2,1)} %reshape.75), calls=%async_computation.1 | async-start | bytes 262144 | tf_op jit(solution)/shard_map/all_to_all | solution.py:54
  183.7 0.3 fusion.6
  184.0 0.0 collective-permute-done.5
  184.0 0.0 collective-permute-done.3
  184.1 0.3 fusion.54
  184.4 15.5 %all-to-all-done.1 = bf16[128,2,192]{2,1,0:T(2,128)(2,1)S(1)} async-done(((bf16[128,2,192]{2,1,0:T(2,128)(2,1)}), bf16[128,2,192]{2,1,0:T(2,128)(2,1)S(1)}, u32[]{:S(2)}, u32[]{:S(2)}) %all-to-all-start.1) | async-done | bytes 98336 | tf_op jit(solution)/shard_map/all_to_all | solution.py:54
  199.9 0.2 reshape.76
  200.1 0.2 convolution_convert_fusion
  200.3 0.1 copy.132
  200.4 0.5 fusion.11
  200.9 0.3 fusion.7
  201.3 0.3 fusion.9
  201.5 0.3 fusion.4
  201.8 0.5 convolution_bitcast_fusion
  202.3 0.8 copy.153
  203.1 0.1 fusion.52
  203.1 0.1 copy.147
  203.2 3.1 %collective-permute-start.8 = (f32[128,384]{0,1:T(8,128)S(1)}, f32[128,384]{0,1:T(8,128)S(1)}, u32[]{:S(2)}, u32[]{:S(2)}) collective-permute-start(f32[128,384]{0,1:T(8,128)S(1)} %bitcast.79), channel_id=1, source_target_pairs={{32,0},{40,8},{48,16},{56,24},{64,32},{72,40},{80,48},{88,56},{96,... | collective-permute-start | bytes 589832 | tf_op jit(solution)/shard_map/ppermute | solution.py:16
  206.3 0.1 copy.146
  206.4 1.9 collective-permute-start.7
  208.4 0.1 copy.145
  208.5 2.6 %collective-permute-start.6 = (f32[128,384]{0,1:T(8,128)S(1)}, f32[128,384]{0,1:T(8,128)S(1)}, u32[]{:S(2)}, u32[]{:S(2)}) collective-permute-start(f32[128,384]{0,1:T(8,128)S(1)} %bitcast.80), channel_id=1, source_target_pairs={{8,0},{16,8},{24,16},{32,24},{40,32},{48,40},{56,48},{64,56},{72,6... | collective-permute-start | bytes 589832 | tf_op jit(solution)/shard_map/ppermute | solution.py:16
  211.1 0.1 copy.144
  211.2 0.1 fusion.51
  211.3 0.1 copy.152
  211.4 1.9 collective-permute-start.11
  213.3 0.1 copy.151
  213.5 1.9 collective-permute-start.10
  215.4 0.1 copy.150
  215.5 0.1 copy.149
  215.7 1.9 collective-permute-start.9
  217.6 0.2 collective-permute-done.7
  217.9 7.0 %collective-permute-done.6 = f32[128,384]{0,1:T(8,128)S(1)} collective-permute-done((f32[128,384]{0,1:T(8,128)S(1)}, f32[128,384]{0,1:T(8,128)S(1)}, u32[]{:S(2)}, u32[]{:S(2)}) %collective-permute-start.6) | collective-permute-done | bytes 196640 | tf_op jit(solution)/shard_map/ppermute | solution.py:16
  224.9 0.8 copy.154
  225.7 1.8 collective-permute-done.10
  227.5 4.5 %collective-permute-done.9 = f32[128,384]{1,0:T(8,128)S(1)} collective-permute-done((f32[128,384]{1,0:T(8,128)S(1)}, f32[128,384]{1,0:T(8,128)S(1)}, u32[]{:S(2)}, u32[]{:S(2)}) %collective-permute-start.9) | collective-permute-done | bytes 196640 | tf_op jit(solution)/shard_map/ppermute | solution.py:16
  232.0 0.7 add_convert_fusion
  (10 shorter events, 0.2 us)
Async XLA Ops:
  7.2 160.1 %all-gather.2.cloned.1.call-start = ((), (), s32[]{:S(2)}) async-start(), calls=%async_computation.2 | async-start | bytes 2377728 | tf_op jit(solution)/shard_map/all_gather | solution.py:30
  8.9 75.1 %collective-permute-start.2 = (bf16[128,384]{0,1:T(8,128)(2,1)S(1)}, bf16[128,384]{0,1:T(8,128)(2,1)S(1)}, u32[]{:S(2)}, u32[]{:S(2)}) collective-permute-start(bf16[128,384]{0,1:T(8,128)(2,1)S(1)} %copy.126), channel_id=1, source_target_pairs={{0,32},{8,40},{16,48},{24,56},{32,64},{40,72},{48,80},{56,88},{64,... | collective-permute-start | bytes 294920 | tf_op jit(solution)/shard_map/ppermute | solution.py:16
  13.8 77.3 %collective-permute-start.1 = (bf16[128,384]{0,1:T(8,128)(2,1)S(1)}, bf16[128,384]{0,1:T(8,128)(2,1)S(1)}, u32[]{:S(2)}, u32[]{:S(2)}) collective-permute-start(bf16[128,384]{0,1:T(8,128)(2,1)S(1)} %copy.126), channel_id=1, source_target_pairs={{0,16},{8,24},{16,32},{24,40},{32,48},{40,56},{48,64},{56,72},{64,... | collective-permute-start | bytes 294920 | tf_op jit(solution)/shard_map/ppermute | solution.py:16
  17.5 73.6 %collective-permute-start = (bf16[128,384]{0,1:T(8,128)(2,1)S(1)}, bf16[128,384]{0,1:T(8,128)(2,1)S(1)}, u32[]{:S(2)}, u32[]{:S(2)}) collective-permute-start(bf16[128,384]{0,1:T(8,128)(2,1)S(1)} %copy.126), channel_id=1, source_target_pairs={{0,8},{8,16},{16,24},{24,32},{32,40},{40,48},{48,56},{56,64},{64,7... | collective-permute-start | bytes 294920 | tf_op jit(solution)/shard_map/ppermute | solution.py:16
  21.9 162.1 %collective-permute-start.5 = (bf16[128,384]{0,1:T(8,128)(2,1)S(1)}, bf16[128,384]{0,1:T(8,128)(2,1)S(1)}, u32[]{:S(2)}, u32[]{:S(2)}) collective-permute-start(bf16[128,384]{0,1:T(8,128)(2,1)S(1)} %copy.136), channel_id=1, source_target_pairs={{0,32},{8,40},{16,48},{24,56},{32,64},{40,72},{48,80},{56,88},{64,... | collective-permute-start | bytes 294920 | tf_op jit(solution)/shard_map/ppermute | solution.py:16
  26.7 157.3 %collective-permute-start.4 = (bf16[128,384]{0,1:T(8,128)(2,1)S(1)}, bf16[128,384]{0,1:T(8,128)(2,1)S(1)}, u32[]{:S(2)}, u32[]{:S(2)}) collective-permute-start(bf16[128,384]{0,1:T(8,128)(2,1)S(1)} %copy.136), channel_id=1, source_target_pairs={{0,16},{8,24},{16,32},{24,40},{32,48},{40,56},{48,64},{56,72},{64,... | collective-permute-start | bytes 294920 | tf_op jit(solution)/shard_map/ppermute | solution.py:16
  34.2 48.7 %all-to-all-start = ((bf16[128,1,1]{2,1,0:T(2,128)(2,1)}), bf16[128,1,1]{2,1,0:T(2,128)(2,1)S(1)}, u32[]{:S(2)}, u32[]{:S(2)}) async-start(bf16[128,1,1]{2,1,0:T(2,128)(2,1)} %copy.130), calls=%async_computation | async-start | bytes 131072 | tf_op jit(solution)/shard_map/all_to_all | solution.py:55
  84.0 100.0 %collective-permute-start.3 = (bf16[128,384]{0,1:T(8,128)(2,1)S(1)}, bf16[128,384]{0,1:T(8,128)(2,1)S(1)}, u32[]{:S(2)}, u32[]{:S(2)}) collective-permute-start(bf16[128,384]{0,1:T(8,128)(2,1)S(1)} %copy.136), channel_id=1, source_target_pairs={{0,8},{8,16},{16,24},{24,32},{32,40},{40,48},{48,56},{56,64},{64,7... | collective-permute-start | bytes 294920 | tf_op jit(solution)/shard_map/ppermute | solution.py:16
  171.6 28.3 %all-to-all-start.1 = ((bf16[128,2,192]{2,1,0:T(2,128)(2,1)}), bf16[128,2,192]{2,1,0:T(2,128)(2,1)S(1)}, u32[]{:S(2)}, u32[]{:S(2)}) async-start(bf16[128,2,192]{2,1,0:T(2,128)(2,1)} %reshape.75), calls=%async_computation.1 | async-start | bytes 262144 | tf_op jit(solution)/shard_map/all_to_all | solution.py:54
  203.2 12.4 %collective-permute-start.8 = (f32[128,384]{0,1:T(8,128)S(1)}, f32[128,384]{0,1:T(8,128)S(1)}, u32[]{:S(2)}, u32[]{:S(2)}) collective-permute-start(f32[128,384]{0,1:T(8,128)S(1)} %bitcast.79), channel_id=1, source_target_pairs={{32,0},{40,8},{48,16},{56,24},{64,32},{72,40},{80,48},{88,56},{96,... | collective-permute-start | bytes 589832 | tf_op jit(solution)/shard_map/ppermute | solution.py:16
  206.4 11.4 %collective-permute-start.7 = (f32[128,384]{0,1:T(8,128)S(1)}, f32[128,384]{0,1:T(8,128)S(1)}, u32[]{:S(2)}, u32[]{:S(2)}) collective-permute-start(f32[128,384]{0,1:T(8,128)S(1)} %bitcast.78), channel_id=1, source_target_pairs={{16,0},{24,8},{32,16},{40,24},{48,32},{56,40},{64,48},{72,56},{80,... | collective-permute-start | bytes 589832 | tf_op jit(solution)/shard_map/ppermute | solution.py:16
  208.5 16.4 %collective-permute-start.6 = (f32[128,384]{0,1:T(8,128)S(1)}, f32[128,384]{0,1:T(8,128)S(1)}, u32[]{:S(2)}, u32[]{:S(2)}) collective-permute-start(f32[128,384]{0,1:T(8,128)S(1)} %bitcast.80), channel_id=1, source_target_pairs={{8,0},{16,8},{24,16},{32,24},{40,32},{48,40},{56,48},{64,56},{72,6... | collective-permute-start | bytes 589832 | tf_op jit(solution)/shard_map/ppermute | solution.py:16
  211.4 14.3 %collective-permute-start.11 = (f32[128,384]{1,0:T(8,128)S(1)}, f32[128,384]{1,0:T(8,128)S(1)}, u32[]{:S(2)}, u32[]{:S(2)}) collective-permute-start(f32[128,384]{1,0:T(8,128)S(1)} %copy.152), channel_id=1, source_target_pairs={{32,0},{40,8},{48,16},{56,24},{64,32},{72,40},{80,48},{88,56},{96,... | collective-permute-start | bytes 589832 | tf_op jit(solution)/shard_map/ppermute | solution.py:16
  213.5 14.0 %collective-permute-start.10 = (f32[128,384]{1,0:T(8,128)S(1)}, f32[128,384]{1,0:T(8,128)S(1)}, u32[]{:S(2)}, u32[]{:S(2)}) collective-permute-start(f32[128,384]{1,0:T(8,128)S(1)} %copy.151), channel_id=1, source_target_pairs={{16,0},{24,8},{32,16},{40,24},{48,32},{56,40},{64,48},{72,56},{80,... | collective-permute-start | bytes 589832 | tf_op jit(solution)/shard_map/ppermute | solution.py:16
  215.7 16.4 %collective-permute-start.9 = (f32[128,384]{1,0:T(8,128)S(1)}, f32[128,384]{1,0:T(8,128)S(1)}, u32[]{:S(2)}, u32[]{:S(2)}) collective-permute-start(f32[128,384]{1,0:T(8,128)S(1)} %copy.149), channel_id=1, source_target_pairs={{8,0},{16,8},{24,16},{32,24},{40,32},{48,40},{56,48},{64,56},{72,6... | collective-permute-start | bytes 589832 | tf_op jit(solution)/shard_map/ppermute | solution.py:16
Sparse Core Ops, SparseCore 0:
  12.2 155.0 all-gather.1
where the time goes:
time: 240 us
  waiting for transfers between devices  106 us (44%)
  starting transfers between devices  74.2 us (31%)
  blocking collectives  24.3 us (10%)
  between operations  14.4 us (6%)
  local copies, waits for them, and re-layouts  9.42 us (4%)
  other arithmetic  5.76 us (2%)
  matrix products  5.51 us (2%)
    all_gather x1, waiting for transfers between devices, per_device(): lax.all_gather(out_weight, 'seq', axis=1, tiled=True)  76.1 us
    ppermute x12, starting transfers between devices, shifted(): return lax.ppermute(value, axis, pairs)  41.4 us
    all_gather x1, blocking collectives, per_device(): full_grad = lax.all_gather(grad_out, 'head', axis=1, tiled=True)  24.3 us
    all_to_all x1, starting transfers between devices, per_device(): lax.all_to_all(slot_pos, 'seq', split_axis=0, concat_axis=0, tiled=True)  20.7 us
    all_to_all x1, waiting for transfers between devices, per_device(): lax.all_to_all(outgoing, 'seq', split_axis=0, concat_axis=0, tiled=True)  15.5 us
    ppermute x12, waiting for transfers between devices, shifted(): return lax.ppermute(value, axis, pairs)  13.6 us
    all_to_all x1, starting transfers between devices, per_device(): lax.all_to_all(outgoing, 'seq', split_axis=0, concat_axis=0, tiled=True)  12.1 us
    unnamed x7, local copies, waits for them, and re-layouts  5.48 us
  transfers between devices with their start and end apart: 15, of which 6 were waited for; matrix products, arithmetic and copies ran while one was open for 7% of the time, Pallas kernels for 0%

commit v1 on v0

v1 whole, which is shorter than its diff:
```python
import jax
import jax.numpy as jnp
from jax import lax
from jax.sharding import Mesh
from jax.sharding import PartitionSpec as P

HEAD_DIM = 128


DISTANCES = (0, 1, 2, 4)
NEG_FILL = -1e30
SEQ = ("z", "x", "core")
F32 = jnp.float32
BF16 = jnp.bfloat16


def shifted(value, by):
    peers = lax.axis_size(SEQ)
    pairs = [(i, i + by) for i in range(peers) if 0 <= i + by < peers]
    return lax.ppermute(value, SEQ, pairs)


def exchange(value, axis):
    return lax.all_to_all(value, axis, split_axis=0, concat_axis=0, tiled=True)


def spread_to(value, axis):
    peers = lax.axis_size(axis)
    return exchange(jnp.broadcast_to(value[None], (peers,) + value.shape), axis)


def three_parts(value):
    high = lax.reduce_precision(value, 8, 7)
    rest = value - high
    middle = lax.reduce_precision(rest, 8, 7)
    return [high.astype(BF16), middle.astype(BF16), (rest - middle).astype(BF16)]


def dot(a, b, dims):
    return lax.dot_general(a, b, (dims, ((), ())), preferred_element_type=F32)


def per_device(
    grad_out, out_weight, row_owner, row_position, query_rows, key_rows, value_rows, band_widths
):
    frame_len = query_rows.shape[0]
    width = query_rows.shape[1]
    heads = width // HEAD_DIM
    scale = HEAD_DIM ** (-0.5)
    frames = lax.axis_size(SEQ)
    frame = lax.axis_index(SEQ)

    w_block = out_weight.T
    w_z = spread_to(w_block, "z")
    w_zx = spread_to(w_z, "x")
    w_all = spread_to(w_zx, "core")
    weight = jnp.transpose(w_all, (2, 1, 0, 3, 4)).reshape(-1, width)

    sel = (row_owner[None, :] == jnp.arange(frames)[:, None]).astype(BF16)
    tagged = jnp.concatenate(
        [grad_out, jnp.broadcast_to(row_position[:, None].astype(BF16), (frame_len, 128))], axis=1
    )
    outgoing = dot(sel, tagged, ((1,), (0,))).astype(BF16)
    incoming = exchange(outgoing.reshape(frames, 1, width + 128), SEQ).reshape(frames, width + 128)
    places = incoming[:, width].astype(F32)
    land = (places[None, :] == jnp.arange(frame_len, dtype=F32)[:, None]).astype(BF16)
    rows = dot(land, incoming[:, :width], ((1,), (0,))).astype(BF16)
    rows_all = spread_to(rows, "head")

    pair = jnp.concatenate([key_rows, value_rows], axis=1)
    pairs_all = [pair] + [shifted(pair, d) for d in DISTANCES[1:]]
    later_queries = [shifted(query_rows, -d) for d in DISTANCES[1:]]

    positions = jnp.arange(frame_len)
    spread = jnp.abs(positions[:, None] - positions[None, :])
    limits = {0: frame_len, 1: frame_len, 2: band_widths[0, 0], 4: band_widths[0, 1]}
    usable = jnp.concatenate(
        [(frame - d >= 0) & (spread < limits[d]) for d in DISTANCES], axis=1
    )

    def head_of(array, h):
        return array[:, h * HEAD_DIM : (h + 1) * HEAD_DIM]

    keys = jnp.concatenate([p[:, :width] for p in pairs_all], axis=0)
    values = jnp.concatenate([p[:, width:] for p in pairs_all], axis=0)
    probs, outs, norms = [], [], []
    for h in range(heads):
        scores = dot(head_of(query_rows, h), head_of(keys, h), ((1,), (1,))) * scale
        row_max = jnp.max(jnp.where(usable, scores, NEG_FILL), axis=1, keepdims=True)
        weights = jnp.where(usable, jnp.exp(scores - row_max), 0.0)
        row_sum = jnp.sum(weights, axis=1, keepdims=True)
        prob = weights / row_sum
        probs.append(prob)
        outs.append(dot(prob.astype(BF16), head_of(values, h), ((1,), (0,))))
        norms.append(row_max + jnp.log(row_sum))
    later_scores = [
        [dot(head_of(q, h), head_of(key_rows, h), ((1,), (1,))) * scale for h in range(heads)]
        for q in later_queries
    ]

    weight = weight.reshape(rows_all.shape[0], width, width)
    grad_attn = lax.dot_general(
        rows_all, weight, (((0, 2), (0, 1)), ((), ())), preferred_element_type=F32
    ).astype(BF16)

    dots = [
        jnp.sum(head_of(grad_attn, h).astype(F32) * outs[h], axis=1, keepdims=True)
        for h in range(heads)
    ]
    tail = three_parts(jnp.concatenate(norms, axis=1)) + three_parts(jnp.concatenate(dots, axis=1))
    tail.append(jnp.broadcast_to(band_widths.astype(BF16), (frame_len, 2)))
    tail.append(jnp.zeros((frame_len, 128 - 6 * heads - 2), BF16))
    parcel = jnp.concatenate([grad_attn] + tail, axis=1)
    later = [shifted(parcel, -d) for d in DISTANCES[1:]]

    grad_query, grad_key, grad_value = [], [], []
    for h in range(heads):
        own_grad = head_of(grad_attn, h)
        grad_prob = dot(own_grad, head_of(values, h), ((1,), (1,)))
        grad_score = (probs[h] * (grad_prob - dots[h])).astype(BF16)
        grad_query.append(scale * dot(grad_score, head_of(keys, h), ((1,), (0,))))
        key_sum = dot(grad_score[:, :frame_len], head_of(query_rows, h), ((0,), (0,)))
        value_sum = dot(probs[h][:, :frame_len].astype(BF16), own_grad, ((0,), (0,)))
        for slot, distance in enumerate(DISTANCES[1:]):
            box = later[slot]
            extra = box[:, width:].astype(F32)
            norm = extra[:, h : h + 1] + extra[:, heads + h : heads + h + 1]
            norm = norm + extra[:, 2 * heads + h : 2 * heads + h + 1]
            first = 3 * heads + h
            row_dot = extra[:, first : first + 1] + extra[:, first + heads : first + heads + 1]
            row_dot = row_dot + extra[:, first + 2 * heads : first + 2 * heads + 1]
            allowed = jnp.broadcast_to(frame + distance < frames, (frame_len, frame_len))
            if distance > 1:
                column = 6 * heads + (0 if distance == 2 else 1)
                allowed = allowed & (spread.astype(F32) < extra[:, column : column + 1])
            prob = jnp.where(
                allowed, jnp.exp(jnp.where(allowed, later_scores[slot][h] - norm, 0.0)), 0.0
            )
            box_grad = head_of(box, h)
            box_prob = dot(box_grad, head_of(value_rows, h), ((1,), (1,)))
            box_score = (prob * (box_prob - row_dot)).astype(BF16)
            key_sum = key_sum + dot(box_score, head_of(later_queries[slot], h), ((0,), (0,)))
            value_sum = value_sum + dot(prob.astype(BF16), box_grad, ((0,), (0,)))
        grad_key.append(scale * key_sum)
        grad_value.append(value_sum)
    return tuple(
        jnp.concatenate(parts, axis=1).astype(BF16) for parts in (grad_query, grad_key, grad_value)
    )


def solution(mesh):
    sizes = {"z": 16, "x": 4, "core": 2}
    grid = mesh.devices.reshape(tuple(sizes.values()) + (mesh.shape["head"],))
    fine = Mesh(grid, tuple(sizes) + ("head",))
    return jax.shard_map(
        per_device,
        mesh=fine,
        in_specs=(
            P(SEQ, "head"),
            P("head", SEQ),
            P(SEQ),
            P(SEQ),
            P(SEQ, "head"),
            P(SEQ, "head"),
            P(SEQ, "head"),
            P(SEQ, None),
        ),
        out_specs=(P(SEQ, "head"), P(SEQ, "head"), P(SEQ, "head")),
        check_vma=False,
    )
```

time: 240 us -> 185 us (0.77)
  the two profiles are of different devices: /device:TPU:7 before, /device:TPU:70 now
where the time goes in v1:
time: 185 us; the launch traced here: 182 us
  starting transfers between devices  78.7 us (43%)
  waiting for transfers between devices  35.1 us (19%)
  matrix products  33.6 us (18%)
  local copies, waits for them, and re-layouts  17.2 us (9%)
  other arithmetic  10.7 us (6%)
  blocking collectives  5.63 us (3%)
    all_to_all x4, starting transfers between devices, exchange(): return lax.all_to_all(value, axis, split_axis=0, concat_axis=0, tiled=True)  47.8 us
    dot_general x47, matrix products, dot(): return lax.dot_general(a, b, (dims, ((), ())), preferred_element_type=F32)  31.3 us
    ppermute x9, starting transfers between devices, shifted(): return lax.ppermute(value, SEQ, pairs)  31 us
    all_to_all x4, waiting for transfers between devices, exchange(): return lax.all_to_all(value, axis, split_axis=0, concat_axis=0, tiled=True)  30.1 us
    all_to_all x1, blocking collectives, exchange(): return lax.all_to_all(value, axis, split_axis=0, concat_axis=0, tiled=True)  5.63 us
    ppermute x9, waiting for transfers between devices, shifted(): return lax.ppermute(value, SEQ, pairs)  5.05 us
    unnamed x67, local copies, waits for them, and re-layouts  4.59 us
    broadcast_in_dim x4, local copies, waits for them, and re-layouts, spread_to(): return exchange(jnp.broadcast_to(value[None], (peers,) + value.shape), axis)  3.74 us
  transfers between devices with their start and end apart: 13, of which 4 were waited for; matrix products, arithmetic and copies ran while one was open for 22% of the time, Pallas kernels for 0%

profile of v1, /device:TPU:70, one launch (start us, length us, event | category | flops | bytes accessed | tf_op | source)
XLA Modules:
  0.0 182.5 jit_solution(2229077191293287073)
XLA Ops:
  0.6 0.7 convert_element_type.158
  1.4 1.1 fusion.10
  3.0 0.7 reduce.42
  3.7 0.7 reshape.114
  4.3 22.1 %all-to-all-start = ((bf16[128,2,256]{2,1,0:T(2,128)(2,1)}), bf16[128,2,256]{2,1,0:T(2,128)(2,1)S(1)}, u32[]{:S(2)}, u32[]{:S(2)}) async-start(bf16[128,2,256]{2,1,0:T(2,128)(2,1)} %reshape.114), calls=%async_computation | async-start | bytes 262144 | tf_op jit(solution)/shard_map/all_to_all | solution.py:24
  26.5 0.9 constant_dynamic-update-slice_fusion.1
  27.4 0.9 constant_dynamic-update-slice_fusion
  28.3 2.0 %collective-permute-start = (bf16[128,768]{1,0:T(8,128)(2,1)S(1)}, bf16[128,768]{1,0:T(8,128)(2,1)S(1)}, u32[]{:S(2)}, u32[]{:S(2)}) collective-permute-start(bf16[128,768]{1,0:T(8,128)(2,1)S(1)} %constant_dynamic-update-slice_fusion), channel_id=1, source_target_pairs={{0,8},{8,16},{16,24},{24,32},{32,40},{40,48},{48,56},{56,64},{64,7... | collective-permute-start | bytes 589832 | tf_op jit(solution)/shard_map/ppermute | solution.py:20
  30.3 3.4 %collective-permute-start.1 = (bf16[128,768]{1,0:T(8,128)(2,1)S(1)}, bf16[128,768]{1,0:T(8,128)(2,1)S(1)}, u32[]{:S(2)}, u32[]{:S(2)}) collective-permute-start(bf16[128,768]{1,0:T(8,128)(2,1)S(1)} %constant_dynamic-update-slice_fusion), channel_id=1, source_target_pairs={{0,16},{8,24},{16,32},{24,40},{32,48},{40,56},{48,64},{56,72},{64,... | collective-permute-start | bytes 589832 | tf_op jit(solution)/shard_map/ppermute | solution.py:20
  33.7 4.3 %collective-permute-start.2 = (bf16[128,768]{1,0:T(8,128)(2,1)S(1)}, bf16[128,768]{1,0:T(8,128)(2,1)S(1)}, u32[]{:S(2)}, u32[]{:S(2)}) collective-permute-start(bf16[128,768]{1,0:T(8,128)(2,1)S(1)} %constant_dynamic-update-slice_fusion), channel_id=1, source_target_pairs={{0,32},{8,40},{16,48},{24,56},{32,64},{40,72},{48,80},{56,88},{64,... | collective-permute-start | bytes 589832 | tf_op jit(solution)/shard_map/ppermute | solution.py:20
  38.0 2.4 %collective-permute-start.3 = (bf16[128,384]{1,0:T(8,128)(2,1)}, bf16[128,384]{1,0:T(8,128)(2,1)}, u32[]{:S(2)}, u32[]{:S(2)}) collective-permute-start(bf16[128,384]{1,0:T(8,128)(2,1)} %param.12), channel_id=1, source_target_pairs={{8,0},{16,8},{24,16},{32,24},{40,32},{48,40},{56,48},{64,56},{72,6... | collective-permute-start | bytes 294920 | tf_op jit(solution)/shard_map/ppermute | solution.py:20
  40.4 4.3 %collective-permute-start.8 = (bf16[128,384]{1,0:T(8,128)(2,1)}, bf16[128,384]{1,0:T(8,128)(2,1)}, u32[]{:S(2)}, u32[]{:S(2)}) collective-permute-start(bf16[128,384]{1,0:T(8,128)(2,1)} %param.12), channel_id=1, source_target_pairs={{32,0},{40,8},{48,16},{56,24},{64,32},{72,40},{80,48},{88,56},{96,... | collective-permute-start | bytes 294920 | tf_op jit(solution)/shard_map/ppermute | solution.py:20
  44.8 1.5 broadcast_in_dim.112
  46.2 11.5 %all-to-all-start.2 = ((bf16[16,24,384]{2,1,0:T(8,128)(2,1)}), bf16[16,24,384]{2,1,0:T(8,128)(2,1)S(1)}, u32[]{:S(2)}, u32[]{:S(2)}) async-start(bf16[16,24,384]{2,1,0:T(8,128)(2,1)} %broadcast_in_dim.112), calls=%async_computation.2 | async-start | bytes 589824 | tf_op jit(solution)/shard_map/all_to_all | solution.py:24
  58.3 1.3 fusion.134
  60.2 5.5 %collective-permute-start.6 = (bf16[128,384]{1,0:T(8,128)(2,1)}, bf16[128,384]{1,0:T(8,128)(2,1)}, u32[]{:S(2)}, u32[]{:S(2)}) collective-permute-start(bf16[128,384]{1,0:T(8,128)(2,1)} %param.12), channel_id=1, source_target_pairs={{16,0},{24,8},{32,16},{40,24},{48,32},{56,40},{64,48},{72,56},{80,... | collective-permute-start | bytes 294920 | tf_op jit(solution)/shard_map/ppermute | solution.py:20
  65.8 10.3 %all-to-all-done.2 = bf16[16,24,384]{2,1,0:T(8,128)(2,1)S(1)} async-done(((bf16[16,24,384]{2,1,0:T(8,128)(2,1)}), bf16[16,24,384]{2,1,0:T(8,128)(2,1)S(1)}, u32[]{:S(2)}, u32[]{:S(2)}) %all-to-all-start.2) | async-done | bytes 294944 | tf_op jit(solution)/shard_map/all_to_all | solution.py:24
  76.1 1.1 broadcast_in_dim.113
  77.2 7.0 %all-to-all-start.3 = ((bf16[4,16,24,384]{3,2,1,0:T(8,128)(2,1)}), bf16[4,16,24,384]{3,2,1,0:T(8,128)(2,1)S(1)}, u32[]{:S(2)}, u32[]{:S(2)}) async-start(bf16[4,16,24,384]{3,2,1,0:T(8,128)(2,1)} %broadcast_in_dim.113), calls=%async_computation.3 | async-start | bytes 2359296 | tf_op jit(solution)/shard_map/all_to_all | solution.py:24
  84.3 0.8 pad_maximum_fusion
  85.1 0.9 fusion.1
  86.1 2.2 %select_reduce_fusion.2 = (f32[128]{0:T(128)}, f32[128,512]{0,1:T(8,128)}) fusion(pred[128,128]{0,1:T(32,128)(4,1)S(1)} %get-tuple-element.68, pred[128,128]{0,1:T(32,128)(4,1)S(1)} %get-tuple-element.67, pred[128,128]{0,1:T(32,128)(4,1)S(1)} %get-tuple-element.65, pred[128,128]{0,1:T(32,128)(4,1)S(1)} %get-tuple-element.66, bf16[128,384]{1,0:T(8,128)(2,1)} %param.12, ...), kind=kOutput, calls=%fused_computation.141 | convolution fusion | flops 17170304 | bytes 492032 | tf_op jit(solution)/shard_map/dot_general | solution.py:40
  88.7 9.1 %all-to-all-done.3 = bf16[4,16,24,384]{3,2,1,0:T(8,128)(2,1)S(1)} async-done(((bf16[4,16,24,384]{3,2,1,0:T(8,128)(2,1)}), bf16[4,16,24,384]{3,2,1,0:T(8,128)(2,1)S(1)}, u32[]{:S(2)}, u32[]{:S(2)}) %all-to-all-start.3) | async-done | bytes 1179680 | tf_op jit(solution)/shard_map/all_to_all | solution.py:24
  98.2 5.6 %all_to_all.25 = bf16[2,4,16,24,384]{4,3,1,2,0:T(8,128)(2,1)S(1)} all-to-all(bf16[2,4,16,24,384]{4,3,1,2,0:T(8,128)(2,1)S(1)} %broadcast_in_dim.114), channel_id=1, replica_groups=mesh['z'=16,'x'=4,'core'=2,'head'=8] {'core'}, dimensions={0} | all-to-all | bytes 4718592 | tf_op jit(solution)/shard_map/all_to_all | solution.py:24
  103.8 1.0 broadcast_in_dim.111
  104.8 7.1 %all-to-all-start.1 = ((bf16[8,128,384]{2,1,0:T(8,128)(2,1)}), bf16[8,128,384]{2,1,0:T(8,128)(2,1)S(1)}, u32[]{:S(2)}, u32[]{:S(2)}) async-start(bf16[8,128,384]{2,1,0:T(8,128)(2,1)} %broadcast_in_dim.111), calls=%async_computation.1 | async-start | bytes 1572864 | tf_op jit(solution)/shard_map/all_to_all | solution.py:24
  111.9 1.3 fusion.90
  113.2 0.7 add_bitcast_fusion.2
  113.9 1.8 fusion.92
  116.8 1.4 copy.137
  118.2 1.4 copy.138
  119.6 1.4 copy.139
  121.0 1.8 fusion.225
  122.8 1.8 copy.129
  124.7 10.6 %all-to-all-done.1 = bf16[8,128,384]{2,1,0:T(8,128)(2,1)S(1)} async-done(((bf16[8,128,384]{2,1,0:T(8,128)(2,1)}), bf16[8,128,384]{2,1,0:T(8,128)(2,1)S(1)}, u32[]{:S(2)}, u32[]{:S(2)}) %all-to-all-start.1) | async-done | bytes 786464 | tf_op jit(solution)/shard_map/all_to_all | solution.py:24
  135.3 2.3 %fusion.9 = bf16[128,384]{1,0:T(8,128)(2,1)S(1)} fusion(bf16[8,128,384]{2,1,0:T(8,128)(2,1)S(1)} %all-to-all-done.1, bf16[8,384,384]{2,1,0:T(8,128)(2,1)} %bitcast.40), kind=kOutput, calls=%fused_computation.17 | convolution fusion | flops 302039040 | bytes 3244032 | tf_op jit(solution)/shard_map/dot_general | solution.py:102
  139.5 1.9 %collective-permute-start.4 = (bf16[128,512]{1,0:T(8,128)(2,1)S(1)}, bf16[128,512]{1,0:T(8,128)(2,1)S(1)}, u32[]{:S(2)}, u32[]{:S(2)}) collective-permute-start(bf16[128,512]{1,0:T(8,128)(2,1)S(1)} %concatenate.44), channel_id=1, source_target_pairs={{8,0},{16,8},{24,16},{32,24},{40,32},{48,40},{56,48},{64,56},{72,6... | collective-permute-start | bytes 393224 | tf_op jit(solution)/shard_map/ppermute | solution.py:20
  141.4 5.1 %collective-permute-start.7 = (bf16[128,512]{1,0:T(8,128)(2,1)S(1)}, bf16[128,512]{1,0:T(8,128)(2,1)S(1)}, u32[]{:S(2)}, u32[]{:S(2)}) collective-permute-start(bf16[128,512]{1,0:T(8,128)(2,1)S(1)} %concatenate.44), channel_id=1, source_target_pairs={{32,0},{40,8},{48,16},{56,24},{64,32},{72,40},{80,48},{88,56},{96,... | collective-permute-start | bytes 393224 | tf_op jit(solution)/shard_map/ppermute | solution.py:20
  147.6 1.0 fusion.148
  148.8 1.0 fusion.146
  150.3 0.8 copy.160
  151.0 1.0 fusion.144
  152.0 2.2 %collective-permute-start.5 = (bf16[128,512]{1,0:T(8,128)(2,1)S(1)}, bf16[128,512]{1,0:T(8,128)(2,1)S(1)}, u32[]{:S(2)}, u32[]{:S(2)}) collective-permute-start(bf16[128,512]{1,0:T(8,128)(2,1)S(1)} %concatenate.44), channel_id=1, source_target_pairs={{16,0},{24,8},{32,16},{40,24},{48,32},{56,40},{64,48},{72,56},{80,... | collective-permute-start | bytes 393224 | tf_op jit(solution)/shard_map/ppermute | solution.py:20
  154.8 0.9 fusion.52
  156.0 5.0 %collective-permute-done.5 = bf16[128,512]{1,0:T(8,128)(2,1)S(1)} collective-permute-done((bf16[128,512]{1,0:T(8,128)(2,1)S(1)}, bf16[128,512]{1,0:T(8,128)(2,1)S(1)}, u32[]{:S(2)}, u32[]{:S(2)}) %collective-permute-start.5) | collective-permute-done | bytes 131104 | tf_op jit(solution)/shard_map/ppermute | solution.py:20
  161.5 0.9 fusion.64
  162.4 0.9 fusion.47
  163.4 0.9 fusion.35
  165.1 0.9 fusion.59
  166.0 0.9 fusion.42
  166.9 0.9 fusion.30
  167.9 0.9 fusion.18
  169.0 0.9 fusion.25
  171.3 0.8 copy.162
  172.0 1.1 fusion.88
  173.1 1.1 fusion.87
  174.2 1.1 fusion.86
  175.2 1.1 convolution_add_fusion.11
  176.3 1.1 convolution_add_fusion.9
  177.4 1.1 convolution_add_fusion.7
  178.5 1.1 fusion.70
  179.6 1.1 fusion.74
  180.6 1.1 fusion.78
  181.7 0.8 copy.161
  (123 shorter events, 10.8 us)
Async XLA Ops:
  0.6 57.1 %copy-start.17 = (s32[1,2]{1,0:T(1,128)S(1)}, s32[1,2]{1,0:T(1,128)}, u32[]{:S(2)}) copy-start(s32[1,2]{1,0:T(1,128)} %param.15) | copy-start | bytes 28
  4.3 40.4 %all-to-all-start = ((bf16[128,2,256]{2,1,0:T(2,128)(2,1)}), bf16[128,2,256]{2,1,0:T(2,128)(2,1)S(1)}, u32[]{:S(2)}, u32[]{:S(2)}) async-start(bf16[128,2,256]{2,1,0:T(2,128)(2,1)} %reshape.114), calls=%async_computation | async-start | bytes 262144 | tf_op jit(solution)/shard_map/all_to_all | solution.py:24
  28.3 31.9 %collective-permute-start = (bf16[128,768]{1,0:T(8,128)(2,1)S(1)}, bf16[128,768]{1,0:T(8,128)(2,1)S(1)}, u32[]{:S(2)}, u32[]{:S(2)}) collective-permute-start(bf16[128,768]{1,0:T(8,128)(2,1)S(1)} %constant_dynamic-update-slice_fusion), channel_id=1, source_target_pairs={{0,8},{8,16},{16,24},{24,32},{32,40},{40,48},{48,56},{56,64},{64,7... | collective-permute-start | bytes 589832 | tf_op jit(solution)/shard_map/ppermute | solution.py:20
  30.3 35.4 %collective-permute-start.1 = (bf16[128,768]{1,0:T(8,128)(2,1)S(1)}, bf16[128,768]{1,0:T(8,128)(2,1)S(1)}, u32[]{:S(2)}, u32[]{:S(2)}) collective-permute-start(bf16[128,768]{1,0:T(8,128)(2,1)S(1)} %constant_dynamic-update-slice_fusion), channel_id=1, source_target_pairs={{0,16},{8,24},{16,32},{24,40},{32,48},{40,56},{48,64},{56,72},{64,... | collective-permute-start | bytes 589832 | tf_op jit(solution)/shard_map/ppermute | solution.py:20
  33.7 32.0 %collective-permute-start.2 = (bf16[128,768]{1,0:T(8,128)(2,1)S(1)}, bf16[128,768]{1,0:T(8,128)(2,1)S(1)}, u32[]{:S(2)}, u32[]{:S(2)}) collective-permute-start(bf16[128,768]{1,0:T(8,128)(2,1)S(1)} %constant_dynamic-update-slice_fusion), channel_id=1, source_target_pairs={{0,32},{8,40},{16,48},{24,56},{32,64},{40,72},{48,80},{56,88},{64,... | collective-permute-start | bytes 589832 | tf_op jit(solution)/shard_map/ppermute | solution.py:20
  38.0 123.5 %collective-permute-start.3 = (bf16[128,384]{1,0:T(8,128)(2,1)}, bf16[128,384]{1,0:T(8,128)(2,1)}, u32[]{:S(2)}, u32[]{:S(2)}) collective-permute-start(bf16[128,384]{1,0:T(8,128)(2,1)} %param.12), channel_id=1, source_target_pairs={{8,0},{16,8},{24,16},{32,24},{40,32},{48,40},{56,48},{64,56},{72,6... | collective-permute-start | bytes 294920 | tf_op jit(solution)/shard_map/ppermute | solution.py:20
  40.4 114.4 %collective-permute-start.8 = (bf16[128,384]{1,0:T(8,128)(2,1)}, bf16[128,384]{1,0:T(8,128)(2,1)}, u32[]{:S(2)}, u32[]{:S(2)}) collective-permute-start(bf16[128,384]{1,0:T(8,128)(2,1)} %param.12), channel_id=1, source_target_pairs={{32,0},{40,8},{48,16},{56,24},{64,32},{72,40},{80,48},{88,56},{96,... | collective-permute-start | bytes 294920 | tf_op jit(solution)/shard_map/ppermute | solution.py:20
  46.2 29.9 %all-to-all-start.2 = ((bf16[16,24,384]{2,1,0:T(8,128)(2,1)}), bf16[16,24,384]{2,1,0:T(8,128)(2,1)S(1)}, u32[]{:S(2)}, u32[]{:S(2)}) async-start(bf16[16,24,384]{2,1,0:T(8,128)(2,1)} %broadcast_in_dim.112), calls=%async_computation.2 | async-start | bytes 589824 | tf_op jit(solution)/shard_map/all_to_all | solution.py:24
  59.6 26.4 %copy-start.12 = (pred[128,128]{0,1:T(32,128)(4,1)}, pred[128,128]{0,1:T(32,128)(4,1)S(1)}, u32[]{:S(2)}) copy-start(pred[128,128]{0,1:T(32,128)(4,1)S(1)} %get-tuple-element.68) | copy-start | bytes 49156
  60.2 104.9 %collective-permute-start.6 = (bf16[128,384]{1,0:T(8,128)(2,1)}, bf16[128,384]{1,0:T(8,128)(2,1)}, u32[]{:S(2)}, u32[]{:S(2)}) collective-permute-start(bf16[128,384]{1,0:T(8,128)(2,1)} %param.12), channel_id=1, source_target_pairs={{16,0},{24,8},{32,16},{40,24},{48,32},{56,40},{64,48},{72,56},{80,... | collective-permute-start | bytes 294920 | tf_op jit(solution)/shard_map/ppermute | solution.py:20
  65.7 18.6 %copy-start = (bf16[128,384]{1,0:T(8,128)(2,1)S(1)}, bf16[128,384]{1,0:T(8,128)(2,1)}, u32[]{:S(2)}) copy-start(bf16[128,384]{1,0:T(8,128)(2,1)} %param.14) | copy-start | bytes 294916
  65.7 18.6 %copy-start.5 = (bf16[128,384]{1,0:T(8,128)(2,1)S(1)}, bf16[128,384]{1,0:T(8,128)(2,1)}, u32[]{:S(2)}) copy-start(bf16[128,384]{1,0:T(8,128)(2,1)} %param.13) | copy-start | bytes 294916
  77.2 20.6 %all-to-all-start.3 = ((bf16[4,16,24,384]{3,2,1,0:T(8,128)(2,1)}), bf16[4,16,24,384]{3,2,1,0:T(8,128)(2,1)S(1)}, u32[]{:S(2)}, u32[]{:S(2)}) async-start(bf16[4,16,24,384]{3,2,1,0:T(8,128)(2,1)} %broadcast_in_dim.113), calls=%async_computation.3 | async-start | bytes 2359296 | tf_op jit(solution)/shard_map/all_to_all | solution.py:24
  85.1 1.0 copy-start.3
  104.8 30.5 %all-to-all-start.1 = ((bf16[8,128,384]{2,1,0:T(8,128)(2,1)}), bf16[8,128,384]{2,1,0:T(8,128)(2,1)S(1)}, u32[]{:S(2)}, u32[]{:S(2)}) async-start(bf16[8,128,384]{2,1,0:T(8,128)(2,1)} %broadcast_in_dim.111), calls=%async_computation.1 | async-start | bytes 1572864 | tf_op jit(solution)/shard_map/all_to_all | solution.py:24
  113.2 0.7 copy-start.1
  113.2 2.5 %copy-start.18 = (f32[128]{0:T(128)}, f32[128]{0:T(128)S(1)}, u32[]{:S(2)}) copy-start(f32[128]{0:T(128)S(1)} %get-tuple-element.40) | copy-start | bytes 1540
  113.2 3.0 %copy-start.22 = (f32[128]{0:T(128)}, f32[128]{0:T(128)S(1)}, u32[]{:S(2)}) copy-start(f32[128]{0:T(128)S(1)} %get-tuple-element.39) | copy-start | bytes 1540
  113.2 3.6 %copy-start.28 = (f32[128]{0:T(128)}, f32[128]{0:T(128)S(1)}, u32[]{:S(2)}) copy-start(f32[128]{0:T(128)S(1)} %get-tuple-element.38) | copy-start | bytes 1540
  115.7 0.5 copy-start.20
  115.7 0.5 copy-start.24
  124.6 13.0 %copy-start.9 = (bf16[128,512]{0,1:T(8,128)(2,1)S(1)}, bf16[128,512]{0,1:T(8,128)(2,1)}, u32[]{:S(2)}) copy-start(bf16[128,512]{0,1:T(8,128)(2,1)} %get-tuple-element.49) | copy-start | bytes 393220
  124.6 13.2 %copy-start.7 = (bf16[512,384]{1,0:T(8,128)(2,1)S(1)}, bf16[512,384]{1,0:T(8,128)(2,1)}, u32[]{:S(2)}) copy-start(bf16[512,384]{1,0:T(8,128)(2,1)} %get-tuple-element.64) | copy-start | bytes 1179652
  124.6 13.6 %copy-start.11 = (bf16[128,512]{0,1:T(8,128)(2,1)S(1)}, bf16[128,512]{0,1:T(8,128)(2,1)}, u32[]{:S(2)}) copy-start(bf16[128,512]{0,1:T(8,128)(2,1)} %get-tuple-element.50) | copy-start | bytes 393220
  124.6 13.9 %copy-start.10 = (bf16[128,512]{0,1:T(8,128)(2,1)S(1)}, bf16[128,512]{0,1:T(8,128)(2,1)}, u32[]{:S(2)}) copy-start(bf16[128,512]{0,1:T(8,128)(2,1)} %get-tuple-element.51) | copy-start | bytes 393220
  124.6 14.6 %copy-start.26 = (bf16[2]{0:T(256)(128)(2,1)S(1)}, bf16[2]{0:T(256)(128)(2,1)}, u32[]{:S(2)}) copy-start(bf16[2]{0:T(256)(128)(2,1)} %convert_bitcast_fusion) | copy-start | bytes 16
  124.6 14.6 %copy-start.14 = (bf16[128,3]{1,0:T(8,128)(2,1)S(1)}, bf16[128,3]{1,0:T(8,128)(2,1)}, u32[]{:S(2)}) copy-start(bf16[128,3]{1,0:T(8,128)(2,1)} %copy.137) | copy-start | bytes 2308
  124.6 14.6 %copy-start.15 = (bf16[128,3]{1,0:T(8,128)(2,1)S(1)}, bf16[128,3]{1,0:T(8,128)(2,1)}, u32[]{:S(2)}) copy-start(bf16[128,3]{1,0:T(8,128)(2,1)} %copy.138) | copy-start | bytes 2308
  124.7 14.6 %copy-start.16 = (bf16[128,3]{1,0:T(8,128)(2,1)S(1)}, bf16[128,3]{1,0:T(8,128)(2,1)}, u32[]{:S(2)}) copy-start(bf16[128,3]{1,0:T(8,128)(2,1)} %copy.139) | copy-start | bytes 2308
  135.3 11.6 %copy-start.8 = (f32[128,512]{0,1:T(8,128)S(1)}, f32[128,512]{0,1:T(8,128)}, u32[]{:S(2)}) copy-start(f32[128,512]{0,1:T(8,128)} %get-tuple-element.61) | copy-start | bytes 786436
  135.3 11.6 %copy-start.13 = (pred[128,128]{0,1:T(32,128)(4,1)S(1)}, pred[128,128]{0,1:T(32,128)(4,1)}, u32[]{:S(2)}) copy-start(pred[128,128]{0,1:T(32,128)(4,1)} %copy-done.12) | copy-start | bytes 49156
  135.3 11.6 %copy-start.27 = (f32[128]{0:T(128)S(1)}, f32[128]{0:T(128)}, u32[]{:S(2)}) copy-start(f32[128]{0:T(128)} %get-tuple-element.60) | copy-start | bytes 1540
  135.3 11.6 %copy-start.29 = (f32[128]{0:T(128)S(1)}, f32[128]{0:T(128)}, u32[]{:S(2)}) copy-start(f32[128]{0:T(128)} %copy-done.28) | copy-start | bytes 1540
  137.6 9.5 %copy-start.2 = (f32[128,512]{0,1:T(8,128)S(1)}, f32[128,512]{0,1:T(8,128)}, u32[]{:S(2)}) copy-start(f32[128,512]{0,1:T(8,128)} %copy-done.1) | copy-start | bytes 786436
  137.6 9.5 %copy-start.23 = (f32[128]{0:T(128)S(1)}, f32[128]{0:T(128)}, u32[]{:S(2)}) copy-start(f32[128]{0:T(128)} %copy-done.22) | copy-start | bytes 1540
  137.6 9.5 %copy-start.25 = (f32[128]{0:T(128)S(1)}, f32[128]{0:T(128)}, u32[]{:S(2)}) copy-start(f32[128]{0:T(128)} %copy-done.24) | copy-start | bytes 1540
  138.8 8.6 %copy-start.19 = (f32[128]{0:T(128)S(1)}, f32[128]{0:T(128)}, u32[]{:S(2)}) copy-start(f32[128]{0:T(128)} %copy-done.18) | copy-start | bytes 1540
  138.8 8.6 %copy-start.21 = (f32[128]{0:T(128)S(1)}, f32[128]{0:T(128)}, u32[]{:S(2)}) copy-start(f32[128]{0:T(128)} %copy-done.20) | copy-start | bytes 1540
  139.5 16.5 %collective-permute-start.4 = (bf16[128,512]{1,0:T(8,128)(2,1)S(1)}, bf16[128,512]{1,0:T(8,128)(2,1)S(1)}, u32[]{:S(2)}, u32[]{:S(2)}) collective-permute-start(bf16[128,512]{1,0:T(8,128)(2,1)S(1)} %concatenate.44), channel_id=1, source_target_pairs={{8,0},{16,8},{24,16},{32,24},{40,32},{48,40},{56,48},{64,56},{72,6... | collective-permute-start | bytes 393224 | tf_op jit(solution)/shard_map/ppermute | solution.py:20
  141.4 10.6 %collective-permute-start.7 = (bf16[128,512]{1,0:T(8,128)(2,1)S(1)}, bf16[128,512]{1,0:T(8,128)(2,1)S(1)}, u32[]{:S(2)}, u32[]{:S(2)}) collective-permute-start(bf16[128,512]{1,0:T(8,128)(2,1)S(1)} %concatenate.44), channel_id=1, source_target_pairs={{32,0},{40,8},{48,16},{56,24},{64,32},{72,40},{80,48},{88,56},{96,... | collective-permute-start | bytes 393224 | tf_op jit(solution)/shard_map/ppermute | solution.py:20
  147.2 1.4 copy-start.4
  147.4 7.4 %copy-start.6 = (bf16[128,384]{1,0:T(8,128)(2,1)S(1)}, bf16[128,384]{1,0:T(8,128)(2,1)}, u32[]{:S(2)}) copy-start(bf16[128,384]{1,0:T(8,128)(2,1)} %param.13) | copy-start | bytes 294916
  152.0 9.0 %collective-permute-start.5 = (bf16[128,512]{1,0:T(8,128)(2,1)S(1)}, bf16[128,512]{1,0:T(8,128)(2,1)S(1)}, u32[]{:S(2)}, u32[]{:S(2)}) collective-permute-start(bf16[128,512]{1,0:T(8,128)(2,1)S(1)} %concatenate.44), channel_id=1, source_target_pairs={{16,0},{24,8},{32,16},{40,24},{48,32},{56,40},{64,48},{72,56},{80,... | collective-permute-start | bytes 393224 | tf_op jit(solution)/shard_map/ppermute | solution.py:20

commit v2 on v1

v2 whole, which is shorter than its diff:
```python
import functools

import jax
import jax.numpy as jnp
from jax import lax
from jax.experimental import pallas as pl
from jax.experimental.pallas import tpu as pltpu
from jax.sharding import Mesh
from jax.sharding import PartitionSpec as P


HEAD_DIM = 128
LANES = 128
DISTANCES = (0, 1, 2, 4)
NEG_FILL = -1e30
SEQ = ("z", "x", "core")
SIZES = {"z": 16, "x": 4, "core": 2}
F32 = jnp.float32
BF16 = jnp.bfloat16
SCALE = HEAD_DIM ** (-0.5)


def shifted(value, by):
    peers = lax.axis_size(SEQ)
    pairs = [(i, i + by) for i in range(peers) if 0 <= i + by < peers]
    return lax.ppermute(value, SEQ, pairs)


def turned(value, axis, by):
    peers = lax.axis_size(axis)
    return lax.ppermute(value, axis, [(i, (i + by) % peers) for i in range(peers)])


def exchange(value, axis):
    return lax.all_to_all(value, axis, split_axis=0, concat_axis=0, tiled=True)


def dot(a, b, left, right):
    return lax.dot_general(a, b, (((left,), (right,)), ((), ())), preferred_element_type=F32)


def call(body, outs, spaces, args, flops):
    smem = pl.BlockSpec(memory_space=pltpu.SMEM)
    vmem = pl.BlockSpec(memory_space=pltpu.VMEM)
    size = sum(a.size * a.dtype.itemsize for a in args)
    size += sum(int(jnp.dtype(t).itemsize) * functools.reduce(lambda m, n: m * n, s) for s, t in outs)
    return pl.pallas_call(
        body,
        out_shape=[jax.ShapeDtypeStruct(s, t) for s, t in outs],
        in_specs=[smem if c == "s" else vmem for c in spaces],
        out_specs=[vmem] * len(outs),
        cost_estimate=pl.CostEstimate(flops=flops, bytes_accessed=size, transcendentals=0),
        compiler_params=pltpu.CompilerParams(vmem_limit_bytes=8 * 2**20),
    )(*args)


def iota(shape, dim):
    return lax.broadcasted_iota(jnp.int32, shape, dim)


def lanes(h):
    return slice(h * LANES, (h + 1) * LANES)


def pack_body(owner, position, grad, weight, key, value, out, pair):
    pick = iota((128, 128), 0) == owner[...]
    place = jnp.sum(jnp.where(pick, position[...].astype(F32), 0.0), axis=1, keepdims=True)
    place = jnp.broadcast_to(place, (128, LANES)).astype(BF16)
    rows = dot(pick.astype(BF16), grad[...], 1, 0).astype(BF16)
    for h in range(3):
        piece = weight[:, lanes(h)]
        for z in range(16):
            out[z, 24 * h : 24 * h + 24, :] = piece
            out[z, 72 + 8 * h : 80 + 8 * h, :] = rows[8 * z : 8 * z + 8, lanes(h)]
    for z in range(16):
        out[z, 96:104, :] = place[8 * z : 8 * z + 8]
    pair[:, :384] = key[...]
    pair[:, 384:] = value[...]


def split_body(got, weight, rows):
    weight[...] = got[:, :72, :]
    row, col = iota((128, 128), 0), iota((128, 128), 1)
    order = (col == (row & 15) * 8 + (row >> 4)).astype(BF16)
    for b in range(4):
        block = got[:, 72 + 8 * b : 80 + 8 * b, :].reshape(128, LANES)
        rows[:, :, lanes(b)] = dot(order, block, 1, 0).astype(BF16).reshape(8, 16, LANES)


def land_body(got, out):
    flat = got[...].reshape(128, 512)
    where = (flat[:, 384:].astype(F32) == iota((128, 128), 1).astype(F32)).astype(BF16)
    rows = dot(where, flat[:, :384], 0, 0).astype(BF16)
    for y in range(8):
        out[y] = rows


def forward_body(frame, band, query, key, value, b1, b2, b4, l1, l2, l4, prob, norm, score):
    spread = jnp.abs(iota((128, 128), 0) - iota((128, 128), 1))
    f = frame[0]
    limits = [
        None,
        jnp.where(f >= 1, 128, 0),
        jnp.where(f >= 2, band[0, 0], 0),
        jnp.where(f >= 4, band[0, 1], 0),
    ]
    for h in range(3):
        q = query[:, lanes(h)]
        parts = []
        for keys, limit in zip((key, b1, b2, b4), limits):
            s = dot(keys[:, lanes(h)], q, 1, 1) * SCALE
            parts.append(s if limit is None else jnp.where(spread < limit, s, NEG_FILL))
        s = jnp.concatenate(parts, axis=0)
        top = jnp.max(s, axis=0, keepdims=True)
        w = jnp.exp(s - top)
        total = jnp.sum(w, axis=0, keepdims=True)
        prob[h] = w / total
        norm[:, lanes(h)] = top + jnp.log(total)
        for i, later in enumerate((l1, l2, l4)):
            score[3 * i + h] = dot(key[:, lanes(h)], later[:, lanes(h)], 1, 1) * SCALE


def gather_body(frame, o0, o1, o2, o3, p0, p1, p2, p3, out):
    x, core = (frame[0] >> 1) & 3, frame[0] & 1
    for c, pieces in enumerate(((o0, o1, o2, o3), (p0, p1, p2, p3))):
        to_core = core if c == 0 else 1 - core
        for turn, piece in enumerate(pieces):
            to_x = (x + 4 - turn) & 3
            for h in range(3):
                out[:, to_x, to_core, :, lanes(h)] = piece[:, 24 * h : 24 * h + 24, :]


def parts_of(value):
    high = value.astype(BF16)
    rest = value - high.astype(F32)
    middle = rest.astype(BF16)
    return high, middle, (rest - middle.astype(F32)).astype(BF16)


def project_body(band, rows, weight, value, b1, b2, b4, prob, norm, parcel, row_dot):
    total = dot(rows[0], weight[0], 1, 0)
    for y in range(1, 8):
        total = total + dot(rows[y], weight[y], 1, 0)
    grad = total.astype(BF16)
    parcel[:128, :] = grad
    dots = []
    for h in range(3):
        g = grad[:, lanes(h)]
        whole = jnp.zeros((1, 128), F32)
        for i, values in enumerate((value, b1, b2, b4)):
            v = values[:, lanes(h)] if i == 0 else values[:, lanes(3 + h)]
            part = prob[h, 128 * i : 128 * i + 128].astype(BF16).astype(F32) * dot(v, g, 1, 1)
            whole = whole + jnp.sum(part, axis=0, keepdims=True)
        dots.append(whole)
    dots = jnp.concatenate(dots, axis=1)
    row_dot[...] = dots
    bands = [jnp.full((1, 384), band[0, i], jnp.int32).astype(F32) for i in range(2)]
    stack = [v.astype(F32) for v in parts_of(norm[...]) + parts_of(dots)] + bands
    parcel[128:, :] = jnp.concatenate(stack, axis=0).astype(BF16)


def own_body(parcel, row_dot, prob, query, key, value, b1, b2, b4, grad_query, key_part, value_part):
    for h in range(3):
        g = parcel[:128, lanes(h)]
        q = query[:, lanes(h)]
        total = None
        for i, pair in enumerate((None, b1, b2, b4)):
            k = key[:, lanes(h)] if i == 0 else pair[:, lanes(h)]
            v = value[:, lanes(h)] if i == 0 else pair[:, lanes(3 + h)]
            p = prob[h, 128 * i : 128 * i + 128]
            s = (p * (dot(v, g, 1, 1) - row_dot[:, lanes(h)])).astype(BF16)
            part = dot(s, k, 0, 0)
            total = part if total is None else total + part
            if i == 0:
                key_part[:, lanes(h)] = dot(s, q, 1, 0)
                value_part[:, lanes(h)] = dot(p.astype(BF16), g, 1, 0)
        grad_query[:, lanes(h)] = (SCALE * total).astype(BF16)


def later_body(frame, a1, a2, a4, l1, l2, l4, score, value, key_part, value_part, grad_key, grad_value):
    spread = jnp.abs(iota((128, 128), 0) - iota((128, 128), 1)).astype(F32)
    for h in range(3):
        keys, values = key_part[:, lanes(h)], value_part[:, lanes(h)]
        for i, (d, box, later) in enumerate(((1, a1, l1), (2, a2, l2), (4, a4, l4))):
            extra = box[128:, lanes(h)].astype(F32)
            norm = extra[0:1] + extra[1:2] + extra[2:3]
            row_dot = extra[3:4] + extra[4:5] + extra[5:6]
            limit = jnp.full((1, 128), 128.0, F32) if d == 1 else extra[5 + d // 2 : 6 + d // 2]
            limit = jnp.where(frame[0] + d < 128, limit, 0.0)
            p = jnp.where(spread < limit, jnp.exp(score[3 * i + h] - norm), 0.0)
            g = box[:128, lanes(h)]
            s = (p * (dot(value[:, lanes(h)], g, 1, 1) - row_dot)).astype(BF16)
            keys = keys + dot(s, later[:, lanes(h)], 1, 0)
            values = values + dot(p.astype(BF16), g, 1, 0)
        grad_key[:, lanes(h)] = (SCALE * keys).astype(BF16)
        grad_value[:, lanes(h)] = values.astype(BF16)


def step(
    grad_out, out_weight, row_owner, row_position, query_rows, key_rows, value_rows, band_widths
):
    frame = lax.axis_index(SEQ).reshape(1)

    packed, pair = call(
        pack_body,
        [((16, 104, LANES), BF16), ((128, 768), BF16)],
        "vvvvvv",
        (row_owner[None], row_position[None], grad_out, out_weight.T, key_rows, value_rows),
        13_000_000,
    )
    got = exchange(packed, "z")
    pairs, later = [], []
    for d in DISTANCES[1:]:
        pairs.append(shifted(pair, d))
    for d in DISTANCES[1:]:
        later.append(shifted(query_rows, -d))
    prob, norm, score = call(
        forward_body,
        [((3, 512, 128), F32), ((1, 384), F32), ((9, 128, 128), F32)],
        "ss" + "v" * 9,
        (frame, band_widths, query_rows, key_rows, value_rows, *pairs, *later),
        90_000_000,
    )
    got, prob, norm, score = lax.optimization_barrier((got, prob, norm, score))

    own, rows = call(split_body, [((16, 72, LANES), BF16), ((8, 16, 512), BF16)], "v", (got,), 17_000_000)
    rows = exchange(rows, ("x", "core"))
    (rows,) = call(land_body, [((8, 128, 384), BF16)], "v", (rows,), 13_000_000)
    rows = exchange(rows, "head")

    right = turned(own, "x", 1)
    left = turned(own, "x", -1)
    far = turned(right, "x", 1)
    pieces = [own, right, far, left]
    swapped = []
    for piece in pieces:
        swapped.append(turned(piece, "core", 1))
    (weight,) = call(gather_body, [((16, 4, 2, 24, 384), BF16)], "s" + "v" * 8, (frame, *pieces, *swapped), 0)
    rows, weight = lax.optimization_barrier((rows, weight))

    parcel, row_dot = call(
        project_body,
        [((136, 384), BF16), ((1, 384), F32)],
        "s" + "v" * 8,
        (band_widths, rows, weight.reshape(8, 384, 384), value_rows, *pairs, prob, norm),
        350_000_000,
    )
    boxes = []
    for d in DISTANCES[1:]:
        boxes.append(shifted(parcel, -d))
    grad_query, key_part, value_part = call(
        own_body,
        [((128, 384), BF16), ((128, 384), F32), ((128, 384), F32)],
        "v" * 9,
        (parcel, row_dot, prob, query_rows, key_rows, value_rows, *pairs),
        120_000_000,
    )
    grad_key, grad_value = call(
        later_body,
        [((128, 384), BF16), ((128, 384), BF16)],
        "s" + "v" * 10,
        (frame, *boxes, *later, score, value_rows, key_part, value_part),
        120_000_000,
    )
    return grad_query, grad_key, grad_value


def solution(mesh):
    grid = mesh.devices.reshape(tuple(SIZES.values()) + (mesh.shape["head"],))
    fine = Mesh(grid, tuple(SIZES) + ("head",))
    return jax.shard_map(
        step,
        mesh=fine,
        in_specs=(
            P(SEQ, "head"),
            P("head", SEQ),
            P(SEQ),
            P(SEQ),
            P(SEQ, "head"),
            P(SEQ, "head"),
            P(SEQ, "head"),
            P(SEQ, None),
        ),
        out_specs=(P(SEQ, "head"), P(SEQ, "head"), P(SEQ, "head")),
        check_vma=False,
    )
```

time: 185 us -> 127 us (0.69)
  the two profiles are of different devices: /device:TPU:70 before, /device:TPU:7 now
where the time goes in v2:
time: 127 us; the launch traced here: 125 us
  starting transfers between devices  76.6 us (60%)
  waiting for transfers between devices  18.4 us (14%)
  local copies, waits for them, and re-layouts  11.8 us (9%)
  Pallas kernels  9.54 us (8%)
  blocking collectives  7.59 us (6%)
    ppermute x9, starting transfers between devices, shifted(): return lax.ppermute(value, SEQ, pairs)  30.2 us
    all_to_all x2, starting transfers between devices, exchange(): return lax.all_to_all(value, axis, split_axis=0, concat_axis=0, tiled=True)  25.4 us
    ppermute x7, starting transfers between devices, turned(): lax.ppermute(value, axis, [(i, (i + by) % peers) for i in range(peers)])  21 us
    ppermute x9, waiting for transfers between devices, shifted(): return lax.ppermute(value, SEQ, pairs)  13.1 us
    unnamed x56, local copies, waits for them, and re-layouts  11.8 us
    pallas_call x8, Pallas kernels, call(): pl.pallas_call(body, out_shape=[jax.ShapeDtypeStruct(s, t) for s, t in ou...  9.54 us
    all_to_all x1, blocking collectives, exchange(): return lax.all_to_all(value, axis, split_axis=0, concat_axis=0, tiled=True)  7.59 us
    ppermute x7, waiting for transfers between devices, turned(): lax.ppermute(value, axis, [(i, (i + by) % peers) for i in range(peers)])  5.27 us
  transfers between devices with their start and end apart: 18, of which 5 were waited for; matrix products, arithmetic and copies ran while one was open for 0% of the time, Pallas kernels for 3%

profile of v2, /device:TPU:7, one launch (start us, length us, event | category | flops | bytes accessed | tf_op | source)
XLA Modules:
  0.0 125.0 jit_solution(10977205917906954763)
XLA Ops:
  0.6 0.0 copy-start
  0.6 0.9 copy-done
  1.5 0.9 copy-done.7
  2.4 0.9 copy-done.22
  3.3 0.7 copy-done.23
  4.0 0.7 copy-done.26
  4.7 0.7 copy-done.27
  5.3 0.9 shard_map.103
  6.3 18.6 %all-to-all-start = ((bf16[16,104,128]{2,1,0:T(8,128)(2,1)}), bf16[16,104,128]{2,1,0:T(8,128)(2,1)S(1)}, u32[]{:S(2)}, u32[]{:S(2)}) async-start(bf16[16,104,128]{2,1,0:T(8,128)(2,1)} %get-tuple-element.23), calls=%async_computation | async-start | bytes 851968 | tf_op jit(solution)/shard_map/all_to_all | solution.py:35
  24.9 3.0 %collective-permute-start.5 = (bf16[128,384]{1,0:T(8,128)(2,1)}, bf16[128,384]{1,0:T(8,128)(2,1)S(1)}, u32[]{:S(2)}, u32[]{:S(2)}) collective-permute-start(bf16[128,384]{1,0:T(8,128)(2,1)} %query.3), channel_id=1, source_target_pairs={{32,0},{40,8},{48,16},{56,24},{64,32},{72,40},{80,48},{88,56},{96,... | collective-permute-start | bytes 294920 | tf_op jit(solution)/shard_map/ppermute | solution.py:26
  27.9 4.7 %collective-permute-start.2 = (bf16[128,768]{1,0:T(8,128)(2,1)S(1)}, bf16[128,768]{1,0:T(8,128)(2,1)S(1)}, u32[]{:S(2)}, u32[]{:S(2)}) collective-permute-start(bf16[128,768]{1,0:T(8,128)(2,1)S(1)} %get-tuple-element.24), channel_id=1, source_target_pairs={{0,32},{8,40},{16,48},{24,56},{32,64},{40,72},{48,80},{56,88},{64,... | collective-permute-start | bytes 589832 | tf_op jit(solution)/shard_map/ppermute | solution.py:26
  32.6 2.3 %collective-permute-start.1 = (bf16[128,768]{1,0:T(8,128)(2,1)S(1)}, bf16[128,768]{1,0:T(8,128)(2,1)S(1)}, u32[]{:S(2)}, u32[]{:S(2)}) collective-permute-start(bf16[128,768]{1,0:T(8,128)(2,1)S(1)} %get-tuple-element.24), channel_id=1, source_target_pairs={{0,16},{8,24},{16,32},{24,40},{32,48},{40,56},{48,64},{56,72},{64,... | collective-permute-start | bytes 589832 | tf_op jit(solution)/shard_map/ppermute | solution.py:26
  34.9 5.1 %collective-permute-start = (bf16[128,768]{1,0:T(8,128)(2,1)S(1)}, bf16[128,768]{1,0:T(8,128)(2,1)S(1)}, u32[]{:S(2)}, u32[]{:S(2)}) collective-permute-start(bf16[128,768]{1,0:T(8,128)(2,1)S(1)} %get-tuple-element.24), channel_id=1, source_target_pairs={{0,8},{8,16},{16,24},{24,32},{32,40},{40,48},{48,56},{56,64},{64,7... | collective-permute-start | bytes 589832 | tf_op jit(solution)/shard_map/ppermute | solution.py:26
  40.0 2.2 %collective-permute-start.4 = (bf16[128,384]{1,0:T(8,128)(2,1)}, bf16[128,384]{1,0:T(8,128)(2,1)S(1)}, u32[]{:S(2)}, u32[]{:S(2)}) collective-permute-start(bf16[128,384]{1,0:T(8,128)(2,1)} %query.3), channel_id=1, source_target_pairs={{16,0},{24,8},{32,16},{40,24},{48,32},{56,40},{64,48},{72,56},{80,... | collective-permute-start | bytes 294920 | tf_op jit(solution)/shard_map/ppermute | solution.py:26
  42.1 5.6 %collective-permute-done.5.l4 = bf16[128,384]{1,0:T(8,128)(2,1)S(1)} collective-permute-done((bf16[128,384]{1,0:T(8,128)(2,1)}, bf16[128,384]{1,0:T(8,128)(2,1)S(1)}, u32[]{:S(2)}, u32[]{:S(2)}) %collective-permute-start.5) | collective-permute-done | bytes 98336 | tf_op jit(solution)/shard_map/ppermute | solution.py:26
  47.7 4.0 %collective-permute-start.3 = (bf16[128,384]{1,0:T(8,128)(2,1)}, bf16[128,384]{1,0:T(8,128)(2,1)S(1)}, u32[]{:S(2)}, u32[]{:S(2)}) collective-permute-start(bf16[128,384]{1,0:T(8,128)(2,1)} %query.3), channel_id=1, source_target_pairs={{8,0},{16,8},{24,16},{32,24},{40,32},{48,40},{56,48},{64,56},{72,6... | collective-permute-start | bytes 294920 | tf_op jit(solution)/shard_map/ppermute | solution.py:26
  51.7 0.0 collective-permute-done.4.l2
  51.7 0.0 copy-start.16
  51.8 4.2 %collective-permute-done.3.l1 = bf16[128,384]{1,0:T(8,128)(2,1)S(1)} collective-permute-done((bf16[128,384]{1,0:T(8,128)(2,1)}, bf16[128,384]{1,0:T(8,128)(2,1)S(1)}, u32[]{:S(2)}, u32[]{:S(2)}) %collective-permute-start.3) | collective-permute-done | bytes 98336 | tf_op jit(solution)/shard_map/ppermute | solution.py:26
  56.0 0.0 collective-permute-done.2.b4
  56.0 0.0 collective-permute-done.1.b2
  56.0 0.0 collective-permute-done.b1
  56.0 0.0 copy-start.1
  56.0 1.0 copy-done.1
  57.0 0.9 copy-done.8
  57.9 0.9 copy-done.12
  58.8 0.7 copy-done.24
  59.5 1.2 shard_map.104
  60.7 0.8 copy-done.10
  61.5 0.0 all-to-all-done.got
  61.5 0.2 shard_map.105
  61.7 7.6 %all_to_all.15.got = bf16[8,16,512]{2,1,0:T(8,128)(2,1)S(1)} all-to-all(bf16[8,16,512]{2,1,0:T(8,128)(2,1)S(1)} %get-tuple-element.29), channel_id=1, replica_groups=mesh['z'=16,'x'=4,'core'=2,'head'=8] {'x','core'}, dimensions={0} | all-to-all | bytes 262144 | tf_op jit(solution)/shard_map/all_to_all | solution.py:35
  69.3 1.2 shard_map.106
  70.5 6.8 %all-to-all-start.2 = ((bf16[8,128,384]{2,1,0:T(8,128)(2,1)}), bf16[8,128,384]{2,1,0:T(8,128)(2,1)}, u32[]{:S(2)}, u32[]{:S(2)}) async-start(bf16[8,128,384]{2,1,0:T(8,128)(2,1)} %shard_map.106), calls=%async_computation.2 | async-start | bytes 1572864 | tf_op jit(solution)/shard_map/all_to_all | solution.py:35
  77.3 0.0 copy-start.25
  77.3 0.0 copy-start.2
  77.3 3.8 %collective-permute-start.6 = (bf16[16,72,128]{2,1,0:T(8,128)(2,1)S(1)}, bf16[16,72,128]{2,1,0:T(8,128)(2,1)S(1)}, u32[]{:S(2)}, u32[]{:S(2)}) collective-permute-start(bf16[16,72,128]{2,1,0:T(8,128)(2,1)S(1)} %get-tuple-element.30.o0), channel_id=1, source_target_pairs={{0,16},{16,32},{32,48},{48,0},{1,17},{17,33},{33,49},{49,1},{2,18}... | collective-permute-start | bytes 884744 | tf_op jit(solution)/shard_map/ppermute | solution.py:31
  81.2 1.9 %collective-permute-start.8 = (bf16[16,72,128]{2,1,0:T(8,128)(2,1)S(1)}, bf16[16,72,128]{2,1,0:T(8,128)(2,1)S(1)}, u32[]{:S(2)}, u32[]{:S(2)}) collective-permute-start(bf16[16,72,128]{2,1,0:T(8,128)(2,1)S(1)} %get-tuple-element.30.o0), channel_id=1, source_target_pairs={{0,48},{16,0},{32,16},{48,32},{1,49},{17,1},{33,17},{49,33},{2,50}... | collective-permute-start | bytes 884744 | tf_op jit(solution)/shard_map/ppermute | solution.py:31
  83.1 3.8 %collective-permute-done.6.o1 = bf16[16,72,128]{2,1,0:T(8,128)(2,1)S(1)} collective-permute-done((bf16[16,72,128]{2,1,0:T(8,128)(2,1)S(1)}, bf16[16,72,128]{2,1,0:T(8,128)(2,1)S(1)}, u32[]{:S(2)}, u32[]{:S(2)}) %collective-permute-start.6) | collective-permute-done | bytes 294944 | tf_op jit(solution)/shard_map/ppermute | solution.py:31
  86.9 4.9 %collective-permute-start.7 = (bf16[16,72,128]{2,1,0:T(8,128)(2,1)S(1)}, bf16[16,72,128]{2,1,0:T(8,128)(2,1)S(1)}, u32[]{:S(2)}, u32[]{:S(2)}) collective-permute-start(bf16[16,72,128]{2,1,0:T(8,128)(2,1)S(1)} %collective-permute-done.6.o1), channel_id=1, source_target_pairs={{0,16},{16,32},{32,48},{48,0},{1,17},{17,33},{33,49},{49,1},{2,18}... | collective-permute-start | bytes 884744 | tf_op jit(solution)/shard_map/ppermute | solution.py:31
  91.8 4.1 %collective-permute-start.9 = (bf16[16,72,128]{2,1,0:T(8,128)(2,1)S(1)}, bf16[16,72,128]{2,1,0:T(8,128)(2,1)S(1)}, u32[]{:S(2)}, u32[]{:S(2)}) collective-permute-start(bf16[16,72,128]{2,1,0:T(8,128)(2,1)S(1)} %get-tuple-element.30.o0), channel_id=1, source_target_pairs={{0,8},{8,0},{1,9},{9,1},{2,10},{10,2},{3,11},{11,3},{4,12},{12,4},... | collective-permute-start | bytes 884744 | tf_op jit(solution)/shard_map/ppermute | solution.py:31
  95.9 1.9 %collective-permute-start.10 = (bf16[16,72,128]{2,1,0:T(8,128)(2,1)S(1)}, bf16[16,72,128]{2,1,0:T(8,128)(2,1)S(1)}, u32[]{:S(2)}, u32[]{:S(2)}) collective-permute-start(bf16[16,72,128]{2,1,0:T(8,128)(2,1)S(1)} %collective-permute-done.6.o1), channel_id=1, source_target_pairs={{0,8},{8,0},{1,9},{9,1},{2,10},{10,2},{3,11},{11,3},{4,12},{12,4},... | collective-permute-start | bytes 884744 | tf_op jit(solution)/shard_map/ppermute | solution.py:31
  97.8 0.0 collective-permute-done.8.o3
  97.8 2.4 %collective-permute-start.12 = (bf16[16,72,128]{2,1,0:T(8,128)(2,1)S(1)}, bf16[16,72,128]{2,1,0:T(8,128)(2,1)S(1)}, u32[]{:S(2)}, u32[]{:S(2)}) collective-permute-start(bf16[16,72,128]{2,1,0:T(8,128)(2,1)S(1)} %collective-permute-done.8.o3), channel_id=1, source_target_pairs={{0,8},{8,0},{1,9},{9,1},{2,10},{10,2},{3,11},{11,3},{4,12},{12,4},... | collective-permute-start | bytes 884744 | tf_op jit(solution)/shard_map/ppermute | solution.py:31
  100.3 0.0 collective-permute-done.7.o2
  100.3 1.9 %collective-permute-start.11 = (bf16[16,72,128]{2,1,0:T(8,128)(2,1)S(1)}, bf16[16,72,128]{2,1,0:T(8,128)(2,1)S(1)}, u32[]{:S(2)}, u32[]{:S(2)}) collective-permute-start(bf16[16,72,128]{2,1,0:T(8,128)(2,1)S(1)} %collective-permute-done.7.o2), channel_id=1, source_target_pairs={{0,8},{8,0},{1,9},{9,1},{2,10},{10,2},{3,11},{11,3},{4,12},{12,4},... | collective-permute-start | bytes 884744 | tf_op jit(solution)/shard_map/ppermute | solution.py:31
  102.2 0.0 collective-permute-done.9.p0
  102.2 0.0 collective-permute-done.12.p3
  102.2 0.0 collective-permute-done.10.p1
  102.3 1.5 %collective-permute-done.11.p2 = bf16[16,72,128]{2,1,0:T(8,128)(2,1)S(1)} collective-permute-done((bf16[16,72,128]{2,1,0:T(8,128)(2,1)S(1)}, bf16[16,72,128]{2,1,0:T(8,128)(2,1)S(1)}, u32[]{:S(2)}, u32[]{:S(2)}) %collective-permute-start.11) | collective-permute-done | bytes 294944 | tf_op jit(solution)/shard_map/ppermute | solution.py:31
  103.7 1.0 copy-done.21
  104.7 0.4 shard_map.107
  105.1 0.0 all-to-all-done.2.rows
  105.2 0.9 copy-done.4
  106.1 0.9 copy-done.6
  107.0 0.0 copy-start.19
  107.0 2.4 %shard_map.108 = (bf16[136,384]{1,0:T(8,128)(2,1)S(1)}, f32[1,384]{1,0:T(1,128)S(1)}) custom-call(s32[1,2]{1,0:T(1,128)S(1)} %copy-done.25, bf16[8,128,384]{2,1,0:T(8,128)(2,1)} %all-to-all-done.2.rows, bf16[8,384,384]{2,1,0:T(8,128)(2,1)S(1)} %bitcast.5, bf16[128,384]{1,0:T(8,128)(2,1)S(1)} %copy-done.2, bf16[128,768]{1,0:T(8,128)(2,1)S(1)} %copy-done.6, ...), custom_call_target="tpu_custom_call" | custom-call | flops 350000000 | bytes 4727816 | tf_op jit(solution)/shard_map/pallas_call | solution.py:47
  109.4 2.2 %collective-permute-start.15 = (bf16[136,384]{1,0:T(8,128)(2,1)S(1)}, bf16[136,384]{1,0:T(8,128)(2,1)S(1)}, u32[]{:S(2)}, u32[]{:S(2)}) collective-permute-start(bf16[136,384]{1,0:T(8,128)(2,1)S(1)} %get-tuple-element.35.parcel), channel_id=1, source_target_pairs={{32,0},{40,8},{48,16},{56,24},{64,32},{72,40},{80,48},{88,56},{96,... | collective-permute-start | bytes 313352 | tf_op jit(solution)/shard_map/ppermute | solution.py:26
  111.6 4.0 %collective-permute-start.14 = (bf16[136,384]{1,0:T(8,128)(2,1)S(1)}, bf16[136,384]{1,0:T(8,128)(2,1)S(1)}, u32[]{:S(2)}, u32[]{:S(2)}) collective-permute-start(bf16[136,384]{1,0:T(8,128)(2,1)S(1)} %get-tuple-element.35.parcel), channel_id=1, source_target_pairs={{16,0},{24,8},{32,16},{40,24},{48,32},{56,40},{64,48},{72,56},{80,... | collective-permute-start | bytes 313352 | tf_op jit(solution)/shard_map/ppermute | solution.py:26
  115.6 2.8 %collective-permute-start.13 = (bf16[136,384]{1,0:T(8,128)(2,1)S(1)}, bf16[136,384]{1,0:T(8,128)(2,1)S(1)}, u32[]{:S(2)}, u32[]{:S(2)}) collective-permute-start(bf16[136,384]{1,0:T(8,128)(2,1)S(1)} %get-tuple-element.35.parcel), channel_id=1, source_target_pairs={{8,0},{16,8},{24,16},{32,24},{40,32},{48,40},{56,48},{64,56},{72,6... | collective-permute-start | bytes 313352 | tf_op jit(solution)/shard_map/ppermute | solution.py:26
  118.4 2.0 %shard_map.109 = (bf16[128,384]{1,0:T(8,128)(2,1)}, f32[128,384]{1,0:T(8,128)S(1)}, f32[128,384]{1,0:T(8,128)S(1)}) custom-call(bf16[136,384]{1,0:T(8,128)(2,1)S(1)} %get-tuple-element.35.parcel, f32[1,384]{1,0:T(1,128)S(1)} %get-tuple-element.36.row_dot, f32[3,512,128]{2,1,0:T(8,128)S(1)} %get-tuple-element.33.prob, bf16[128,384]{1,0:T(8,128)(2,1)S(1)} %copy-done.13, ...), custom_call_target="tpu_custom_call" | custom-call | flops 120000000 | bytes 2268672 | tf_op jit(solution)/shard_map/pallas_call | solution.py:47
  120.4 0.0 collective-permute-done.15.a4
  120.4 3.3 %collective-permute-done.13.a1 = bf16[136,384]{1,0:T(8,128)(2,1)S(1)} collective-permute-done((bf16[136,384]{1,0:T(8,128)(2,1)S(1)}, bf16[136,384]{1,0:T(8,128)(2,1)S(1)}, u32[]{:S(2)}, u32[]{:S(2)}) %collective-permute-start.13) | collective-permute-done | bytes 104480 | tf_op jit(solution)/shard_map/ppermute | solution.py:26
  123.7 1.3 %shard_map.110 = (bf16[128,384]{1,0:T(8,128)(2,1)}, bf16[128,384]{1,0:T(8,128)(2,1)}) custom-call(s32[1]{0:T(128)} %bitcast.3.frame, bf16[136,384]{1,0:T(8,128)(2,1)S(1)} %collective-permute-done.13.a1, bf16[136,384]{1,0:T(8,128)(2,1)S(1)} %collective-permute-done.14.a2, bf16[136,384]{1,0:T(8,128)(2,1)S(1)} %collective-permute-done.15.a4, ...), custom_call_target="tpu_custom_call" | custom-call | flops 120000000 | bytes 1886212 | tf_op jit(solution)/shard_map/pallas_call | solution.py:47
  (37 shorter events, 0.1 us)
Async XLA Ops:
  0.6 0.9 copy-start
  1.5 0.9 copy-start.7
  2.4 0.9 copy-start.22
  3.3 0.7 copy-start.23
  4.0 0.7 copy-start.26
  4.7 0.7 copy-start.27
  6.3 55.2 %all-to-all-start = ((bf16[16,104,128]{2,1,0:T(8,128)(2,1)}), bf16[16,104,128]{2,1,0:T(8,128)(2,1)S(1)}, u32[]{:S(2)}, u32[]{:S(2)}) async-start(bf16[16,104,128]{2,1,0:T(8,128)(2,1)} %get-tuple-element.23), calls=%async_computation | async-start | bytes 851968 | tf_op jit(solution)/shard_map/all_to_all | solution.py:35
  24.9 22.9 %collective-permute-start.5 = (bf16[128,384]{1,0:T(8,128)(2,1)}, bf16[128,384]{1,0:T(8,128)(2,1)S(1)}, u32[]{:S(2)}, u32[]{:S(2)}) collective-permute-start(bf16[128,384]{1,0:T(8,128)(2,1)} %query.3), channel_id=1, source_target_pairs={{32,0},{40,8},{48,16},{56,24},{64,32},{72,40},{80,48},{88,56},{96,... | collective-permute-start | bytes 294920 | tf_op jit(solution)/shard_map/ppermute | solution.py:26
  27.9 28.1 %collective-permute-start.2 = (bf16[128,768]{1,0:T(8,128)(2,1)S(1)}, bf16[128,768]{1,0:T(8,128)(2,1)S(1)}, u32[]{:S(2)}, u32[]{:S(2)}) collective-permute-start(bf16[128,768]{1,0:T(8,128)(2,1)S(1)} %get-tuple-element.24), channel_id=1, source_target_pairs={{0,32},{8,40},{16,48},{24,56},{32,64},{40,72},{48,80},{56,88},{64,... | collective-permute-start | bytes 589832 | tf_op jit(solution)/shard_map/ppermute | solution.py:26
  32.6 23.4 %collective-permute-start.1 = (bf16[128,768]{1,0:T(8,128)(2,1)S(1)}, bf16[128,768]{1,0:T(8,128)(2,1)S(1)}, u32[]{:S(2)}, u32[]{:S(2)}) collective-permute-start(bf16[128,768]{1,0:T(8,128)(2,1)S(1)} %get-tuple-element.24), channel_id=1, source_target_pairs={{0,16},{8,24},{16,32},{24,40},{32,48},{40,56},{48,64},{56,72},{64,... | collective-permute-start | bytes 589832 | tf_op jit(solution)/shard_map/ppermute | solution.py:26
  34.9 21.1 %collective-permute-start = (bf16[128,768]{1,0:T(8,128)(2,1)S(1)}, bf16[128,768]{1,0:T(8,128)(2,1)S(1)}, u32[]{:S(2)}, u32[]{:S(2)}) collective-permute-start(bf16[128,768]{1,0:T(8,128)(2,1)S(1)} %get-tuple-element.24), channel_id=1, source_target_pairs={{0,8},{8,16},{16,24},{24,32},{32,40},{40,48},{48,56},{56,64},{64,7... | collective-permute-start | bytes 589832 | tf_op jit(solution)/shard_map/ppermute | solution.py:26
  40.0 11.8 %collective-permute-start.4 = (bf16[128,384]{1,0:T(8,128)(2,1)}, bf16[128,384]{1,0:T(8,128)(2,1)S(1)}, u32[]{:S(2)}, u32[]{:S(2)}) collective-permute-start(bf16[128,384]{1,0:T(8,128)(2,1)} %query.3), channel_id=1, source_target_pairs={{16,0},{24,8},{32,16},{40,24},{48,32},{56,40},{64,48},{72,56},{80,... | collective-permute-start | bytes 294920 | tf_op jit(solution)/shard_map/ppermute | solution.py:26
  47.7 29.6 %copy-start.14 = (bf16[128,384]{1,0:T(8,128)(2,1)}, bf16[128,384]{1,0:T(8,128)(2,1)S(1)}, u32[]{:S(2)}) copy-start(bf16[128,384]{1,0:T(8,128)(2,1)S(1)} %collective-permute-done.5.l4) | copy-start | bytes 294916
  47.7 8.2 %collective-permute-start.3 = (bf16[128,384]{1,0:T(8,128)(2,1)}, bf16[128,384]{1,0:T(8,128)(2,1)S(1)}, u32[]{:S(2)}, u32[]{:S(2)}) collective-permute-start(bf16[128,384]{1,0:T(8,128)(2,1)} %query.3), channel_id=1, source_target_pairs={{8,0},{16,8},{24,16},{32,24},{40,32},{48,40},{56,48},{64,56},{72,6... | collective-permute-start | bytes 294920 | tf_op jit(solution)/shard_map/ppermute | solution.py:26
  51.7 50.5 %copy-start.16 = (bf16[128,384]{1,0:T(8,128)(2,1)}, bf16[128,384]{1,0:T(8,128)(2,1)S(1)}, u32[]{:S(2)}) copy-start(bf16[128,384]{1,0:T(8,128)(2,1)S(1)} %collective-permute-done.4.l2) | copy-start | bytes 294916
  56.0 46.2 %copy-start.18 = (bf16[128,384]{1,0:T(8,128)(2,1)}, bf16[128,384]{1,0:T(8,128)(2,1)S(1)}, u32[]{:S(2)}) copy-start(bf16[128,384]{1,0:T(8,128)(2,1)S(1)} %collective-permute-done.3.l1) | copy-start | bytes 294916
  56.0 46.2 %copy-start.3 = (bf16[128,768]{1,0:T(8,128)(2,1)}, bf16[128,768]{1,0:T(8,128)(2,1)S(1)}, u32[]{:S(2)}) copy-start(bf16[128,768]{1,0:T(8,128)(2,1)S(1)} %collective-permute-done.1.b2) | copy-start | bytes 589828
  56.0 46.2 %copy-start.5 = (bf16[128,768]{1,0:T(8,128)(2,1)}, bf16[128,768]{1,0:T(8,128)(2,1)S(1)}, u32[]{:S(2)}) copy-start(bf16[128,768]{1,0:T(8,128)(2,1)S(1)} %collective-permute-done.b1) | copy-start | bytes 589828
  56.0 1.0 copy-start.1
  57.0 0.9 copy-start.8
  57.9 0.9 copy-start.12
  58.8 0.7 copy-start.24
  60.7 0.8 copy-start.10
  61.7 40.5 %copy-start.20 = (bf16[16,72,128]{2,1,0:T(8,128)(2,1)}, bf16[16,72,128]{2,1,0:T(8,128)(2,1)S(1)}, u32[]{:S(2)}) copy-start(bf16[16,72,128]{2,1,0:T(8,128)(2,1)S(1)} %get-tuple-element.30.o0) | copy-start | bytes 884740
  70.5 34.6 %all-to-all-start.2 = ((bf16[8,128,384]{2,1,0:T(8,128)(2,1)}), bf16[8,128,384]{2,1,0:T(8,128)(2,1)}, u32[]{:S(2)}, u32[]{:S(2)}) async-start(bf16[8,128,384]{2,1,0:T(8,128)(2,1)} %shard_map.106), calls=%async_computation.2 | async-start | bytes 1572864 | tf_op jit(solution)/shard_map/all_to_all | solution.py:35
  77.3 27.8 %copy-start.25 = (s32[1,2]{1,0:T(1,128)S(1)}, s32[1,2]{1,0:T(1,128)}, u32[]{:S(2)}) copy-start(s32[1,2]{1,0:T(1,128)} %band.3) | copy-start | bytes 28
  77.3 27.8 %copy-start.2 = (bf16[128,384]{1,0:T(8,128)(2,1)S(1)}, bf16[128,384]{1,0:T(8,128)(2,1)}, u32[]{:S(2)}) copy-start(bf16[128,384]{1,0:T(8,128)(2,1)} %value.9) | copy-start | bytes 294916
  77.3 9.6 %collective-permute-start.6 = (bf16[16,72,128]{2,1,0:T(8,128)(2,1)S(1)}, bf16[16,72,128]{2,1,0:T(8,128)(2,1)S(1)}, u32[]{:S(2)}, u32[]{:S(2)}) collective-permute-start(bf16[16,72,128]{2,1,0:T(8,128)(2,1)S(1)} %get-tuple-element.30.o0), channel_id=1, source_target_pairs={{0,16},{16,32},{32,48},{48,0},{1,17},{17,33},{33,49},{49,1},{2,18}... | collective-permute-start | bytes 884744 | tf_op jit(solution)/shard_map/ppermute | solution.py:31
  81.2 16.6 %collective-permute-start.8 = (bf16[16,72,128]{2,1,0:T(8,128)(2,1)S(1)}, bf16[16,72,128]{2,1,0:T(8,128)(2,1)S(1)}, u32[]{:S(2)}, u32[]{:S(2)}) collective-permute-start(bf16[16,72,128]{2,1,0:T(8,128)(2,1)S(1)} %get-tuple-element.30.o0), channel_id=1, source_target_pairs={{0,48},{16,0},{32,16},{48,32},{1,49},{17,1},{33,17},{49,33},{2,50}... | collective-permute-start | bytes 884744 | tf_op jit(solution)/shard_map/ppermute | solution.py:31
  86.9 13.4 %collective-permute-start.7 = (bf16[16,72,128]{2,1,0:T(8,128)(2,1)S(1)}, bf16[16,72,128]{2,1,0:T(8,128)(2,1)S(1)}, u32[]{:S(2)}, u32[]{:S(2)}) collective-permute-start(bf16[16,72,128]{2,1,0:T(8,128)(2,1)S(1)} %collective-permute-done.6.o1), channel_id=1, source_target_pairs={{0,16},{16,32},{32,48},{48,0},{1,17},{17,33},{33,49},{49,1},{2,18}... | collective-permute-start | bytes 884744 | tf_op jit(solution)/shard_map/ppermute | solution.py:31
  91.8 10.4 %collective-permute-start.9 = (bf16[16,72,128]{2,1,0:T(8,128)(2,1)S(1)}, bf16[16,72,128]{2,1,0:T(8,128)(2,1)S(1)}, u32[]{:S(2)}, u32[]{:S(2)}) collective-permute-start(bf16[16,72,128]{2,1,0:T(8,128)(2,1)S(1)} %get-tuple-element.30.o0), channel_id=1, source_target_pairs={{0,8},{8,0},{1,9},{9,1},{2,10},{10,2},{3,11},{11,3},{4,12},{12,4},... | collective-permute-start | bytes 884744 | tf_op jit(solution)/shard_map/ppermute | solution.py:31
  95.9 6.3 %collective-permute-start.10 = (bf16[16,72,128]{2,1,0:T(8,128)(2,1)S(1)}, bf16[16,72,128]{2,1,0:T(8,128)(2,1)S(1)}, u32[]{:S(2)}, u32[]{:S(2)}) collective-permute-start(bf16[16,72,128]{2,1,0:T(8,128)(2,1)S(1)} %collective-permute-done.6.o1), channel_id=1, source_target_pairs={{0,8},{8,0},{1,9},{9,1},{2,10},{10,2},{3,11},{11,3},{4,12},{12,4},... | collective-permute-start | bytes 884744 | tf_op jit(solution)/shard_map/ppermute | solution.py:31
  97.8 4.4 %collective-permute-start.12 = (bf16[16,72,128]{2,1,0:T(8,128)(2,1)S(1)}, bf16[16,72,128]{2,1,0:T(8,128)(2,1)S(1)}, u32[]{:S(2)}, u32[]{:S(2)}) collective-permute-start(bf16[16,72,128]{2,1,0:T(8,128)(2,1)S(1)} %collective-permute-done.8.o3), channel_id=1, source_target_pairs={{0,8},{8,0},{1,9},{9,1},{2,10},{10,2},{3,11},{11,3},{4,12},{12,4},... | collective-permute-start | bytes 884744 | tf_op jit(solution)/shard_map/ppermute | solution.py:31
  100.3 3.5 %collective-permute-start.11 = (bf16[16,72,128]{2,1,0:T(8,128)(2,1)S(1)}, bf16[16,72,128]{2,1,0:T(8,128)(2,1)S(1)}, u32[]{:S(2)}, u32[]{:S(2)}) collective-permute-start(bf16[16,72,128]{2,1,0:T(8,128)(2,1)S(1)} %collective-permute-done.7.o2), channel_id=1, source_target_pairs={{0,8},{8,0},{1,9},{9,1},{2,10},{10,2},{3,11},{11,3},{4,12},{12,4},... | collective-permute-start | bytes 884744 | tf_op jit(solution)/shard_map/ppermute | solution.py:31
  103.7 1.0 copy-start.21
  104.7 13.7 %copy-start.9 = (bf16[128,384]{1,0:T(8,128)(2,1)S(1)}, bf16[128,384]{1,0:T(8,128)(2,1)}, u32[]{:S(2)}) copy-start(bf16[128,384]{1,0:T(8,128)(2,1)} %key.5) | copy-start | bytes 294916
  105.1 0.9 copy-start.4
  106.1 0.9 copy-start.6
  107.0 11.4 %copy-start.13 = (bf16[128,384]{1,0:T(8,128)(2,1)S(1)}, bf16[128,384]{1,0:T(8,128)(2,1)}, u32[]{:S(2)}) copy-start(bf16[128,384]{1,0:T(8,128)(2,1)} %query.3) | copy-start | bytes 294916
  107.0 16.7 %copy-start.11 = (f32[9,128,128]{2,1,0:T(8,128)S(1)}, f32[9,128,128]{2,1,0:T(8,128)}, u32[]{:S(2)}) copy-start(f32[9,128,128]{2,1,0:T(8,128)} %copy-done.10) | copy-start | bytes 1769476
  107.0 16.7 %copy-start.15 = (bf16[128,384]{1,0:T(8,128)(2,1)S(1)}, bf16[128,384]{1,0:T(8,128)(2,1)}, u32[]{:S(2)}) copy-start(bf16[128,384]{1,0:T(8,128)(2,1)} %copy-done.14) | copy-start | bytes 294916
  107.0 16.7 %copy-start.17 = (bf16[128,384]{1,0:T(8,128)(2,1)S(1)}, bf16[128,384]{1,0:T(8,128)(2,1)}, u32[]{:S(2)}) copy-start(bf16[128,384]{1,0:T(8,128)(2,1)} %copy-done.16) | copy-start | bytes 294916
  107.0 16.7 %copy-start.19 = (bf16[128,384]{1,0:T(8,128)(2,1)S(1)}, bf16[128,384]{1,0:T(8,128)(2,1)}, u32[]{:S(2)}) copy-start(bf16[128,384]{1,0:T(8,128)(2,1)} %copy-done.18) | copy-start | bytes 294916
  109.4 11.0 %collective-permute-start.15 = (bf16[136,384]{1,0:T(8,128)(2,1)S(1)}, bf16[136,384]{1,0:T(8,128)(2,1)S(1)}, u32[]{:S(2)}, u32[]{:S(2)}) collective-permute-start(bf16[136,384]{1,0:T(8,128)(2,1)S(1)} %get-tuple-element.35.parcel), channel_id=1, source_target_pairs={{32,0},{40,8},{48,16},{56,24},{64,32},{72,40},{80,48},{88,56},{96,... | collective-permute-start | bytes 313352 | tf_op jit(solution)/shard_map/ppermute | solution.py:26
  111.6 8.8 %collective-permute-start.14 = (bf16[136,384]{1,0:T(8,128)(2,1)S(1)}, bf16[136,384]{1,0:T(8,128)(2,1)S(1)}, u32[]{:S(2)}, u32[]{:S(2)}) collective-permute-start(bf16[136,384]{1,0:T(8,128)(2,1)S(1)} %get-tuple-element.35.parcel), channel_id=1, source_target_pairs={{16,0},{24,8},{32,16},{40,24},{48,32},{56,40},{64,48},{72,56},{80,... | collective-permute-start | bytes 313352 | tf_op jit(solution)/shard_map/ppermute | solution.py:26
  115.6 8.1 %collective-permute-start.13 = (bf16[136,384]{1,0:T(8,128)(2,1)S(1)}, bf16[136,384]{1,0:T(8,128)(2,1)S(1)}, u32[]{:S(2)}, u32[]{:S(2)}) collective-permute-start(bf16[136,384]{1,0:T(8,128)(2,1)S(1)} %get-tuple-element.35.parcel), channel_id=1, source_target_pairs={{8,0},{16,8},{24,16},{32,24},{40,32},{48,40},{56,48},{64,56},{72,6... | collective-permute-start | bytes 313352 | tf_op jit(solution)/shard_map/ppermute | solution.py:26
